TPU v7x, 32 devices: a whole 2x2x4 slice. The times are simulated.
32 devices in a mesh: gx: 4 (over y, x), gy: 8 (over z, core).
Axes of the slice: x: 2, y: 2, z: 4, core: 2. Of those that a mesh axis runs over, the one named last changes fastest.
Arguments:
- adjoint_temp: float32 [128, 256, 256], P('gx', 'gy'), may hold values from -6 to 6
- adjoint_load: float32 [128, 256, 256], P('gx', 'gy'), may hold values from -6 to 6
- conductivity: float32 [3, 128, 256, 256], P(None, 'gx', 'gy'), may hold values from 0.25 to 4
- expansion: float32 [3, 128, 256, 256], P(None, 'gx', 'gy'), may hold values from 0.5 to 2
- ref_temp: float32 [128, 256, 256], P('gx', 'gy'), may hold values from -4 to 4
- wall_rows: float32 [8192, 128], P(('gx', 'gy')), may hold values from -6 to 6
- wall_dest: int32 [8192, 1], P(('gx', 'gy')), may hold values from 0 to 31; in each aligned block of 256 rows (0 to 255, 256 to 511, ...) at most 9 rows name the same one
- wall_line: int32 [8192], P(('gx', 'gy')), may hold values from 0 to 2047
- wall_count: int32 [32], P(('gx', 'gy')), may hold values from 192 to 256, as said below
- tile_owner: int32 [32, 32], P(('gx', 'gy')), may hold values from 0 to 31, each once within a row
Outputs:
- adjoint_field: float32 [128, 256, 256], P('gx', 'gy')
- block_load: float32 [32, 3, 32, 8192], P(('gx', 'gy'))
Inputs may be any that keep to these rules, and one draw needn't show every extreme that they name: Each row of tile_owner names every elasticity block once. `wall_dest`: bricks are numbered with the span index slowest. Among the 256 row slots of one device, no brick is named by more than 9 of them. `wall_count`: some device has all 256 slots live.
All inputs are finite; a program needn't handle non-finite values.
Results may differ from a plain program's by a relative error of at most 0.0003.
Values sent between devices are 32-bit elements; how exact they have to be, the bound alone decides.
No kernel may reach another device: no remote copies, remote signals or barrier semaphores. Data moves between devices by JAX's collectives and lax.ppermute only.
A program may use at most 128 MiB of HBM per device.

v0:
```python
from functools import reduce

import jax
import jax.numpy as jnp
from jax import lax
from jax.sharding import PartitionSpec as P

OMEGA = 0.8
CLASS_WEIGHTS = (1.0, 0.25, 0.125)


def padded_2(block, sides, width):
    for axis, dim in sides:
        count = lax.axis_size(axis)
        forward = [(i, i + 1) for i in range(count - 1)]
        backward = [(target, source) for source, target in forward]
        low = lax.ppermute(
            lax.slice_in_dim(block, block.shape[dim] - width, None, axis=dim), axis, forward
        )
        high = lax.ppermute(lax.slice_in_dim(block, 0, width, axis=dim), axis, backward)
        block = jnp.concatenate([low, block, high], axis=dim)
    return block


def sweep(field_pad, conduct_pad, source, inside):
    padded = jnp.pad(field_pad, ((0, 0), (0, 0), (1, 1)))
    conduct = jnp.pad(conduct_pad, ((0, 0), (0, 0), (0, 0), (1, 1)))
    size_x = padded.shape[0] - 2
    size_y = padded.shape[1] - 2
    size_z = padded.shape[2] - 2
    center = padded[1:-1, 1:-1, 1:-1]
    coupled = jnp.zeros(center.shape, jnp.float32)
    diagonal = jnp.zeros(center.shape, jnp.float32)
    blends = {}
    for shift_x in (-1, 0, 1):
        for shift_y in (-1, 0, 1):
            for shift_z in (-1, 0, 1):
                shifts = (shift_x, shift_y, shift_z)
                axes_set = tuple((a for a in range(3) if shifts[a] != 0))
                if len(axes_set) == 0:
                    continue
                if axes_set not in blends:
                    blends[axes_set] = reduce(
                        lambda left, right: left + right, [conduct[a] for a in axes_set]
                    ) / float(len(axes_set))
                blended = blends[axes_set]
                local_k = blended[1:-1, 1:-1, 1:-1]
                across = lax.slice(
                    blended,
                    (1 + shift_x, 1 + shift_y, 1 + shift_z),
                    (1 + shift_x + size_x, 1 + shift_y + size_y, 1 + shift_z + size_z),
                )
                neighbour = lax.slice(
                    padded,
                    (1 + shift_x, 1 + shift_y, 1 + shift_z),
                    (1 + shift_x + size_x, 1 + shift_y + size_y, 1 + shift_z + size_z),
                )
                coupling = 0.5 * CLASS_WEIGHTS[len(axes_set) - 1] * (local_k + across)
                coupled = coupled + coupling * (center - neighbour)
                diagonal = diagonal + coupling
    applied = center + coupled
    return (center + OMEGA * (source - applied) / (1.0 + diagonal)) * inside


def exchange_rim(stacked, width):
    return padded_2(stacked, (("gx", 1), ("gy", 2)), width)


def body(
    adjoint_temp,
    adjoint_load,
    conductivity,
    expansion,
    ref_temp,
    wall_rows,
    wall_dest,
    wall_line,
    wall_count,
    tile_owner,
):
    span_count = lax.axis_size("gx")
    column_count = lax.axis_size("gy")
    devices = span_count * column_count
    size_x, size_y, size_z = adjoint_temp.shape
    rows_dev, row_width = wall_rows.shape
    segments = size_x * size_y * size_z // row_width
    capacity = (rows_dev + devices - 1) // devices + 1
    position = jnp.arange(rows_dev, dtype=jnp.int32)
    live = position < wall_count[0]
    target_brick = wall_dest[:, 0]
    labels = jnp.arange(devices, dtype=jnp.int32)
    onehot = ((target_brick[:, None] == labels[None, :]) & live[:, None]).astype(jnp.int32)
    earlier = jnp.cumsum(onehot, axis=0) - onehot
    slot_index = jnp.sum(earlier * onehot, axis=1)
    target = jnp.where(live, target_brick * capacity + slot_index, devices * capacity)
    send_rows = (
        jnp.zeros((devices * capacity, row_width), jnp.float32)
        .at[target]
        .set(wall_rows, mode="drop")
    )
    send_lines = (
        jnp.full((devices * capacity,), segments, jnp.int32).at[target].set(wall_line, mode="drop")
    )
    got_rows, got_lines = (
        lax.all_to_all(
            send_rows.reshape(devices, capacity, row_width),
            ("gx", "gy"),
            split_axis=0,
            concat_axis=0,
            tiled=True,
        ),
        lax.all_to_all(
            send_lines.reshape(devices, capacity),
            ("gx", "gy"),
            split_axis=0,
            concat_axis=0,
            tiled=True,
        ),
    )
    source = (
        adjoint_load.reshape(segments, row_width)
        .at[got_lines.reshape(-1)]
        .add(got_rows.reshape(-1, row_width), mode="drop")
        .reshape(size_x, size_y, size_z)
    )
    stacked = jnp.concatenate([adjoint_temp[None], conductivity], axis=0)
    padded = exchange_rim(stacked, 1)
    first = sweep(padded[0], padded[1:], source, 1.0)
    first_pad = exchange_rim(first[None], 1)[0]
    adjoint_field = sweep(first_pad, padded[1:], source, 1.0)
    thermal_load = expansion * (adjoint_field - ref_temp)[None]
    tile_cells = size_x * size_y * size_z // devices
    tiles = thermal_load.reshape(3, devices, tile_cells)
    matches = (tile_owner[0][:, None] == labels[None, :]).astype(jnp.int32)
    inverse = jnp.sum(matches * labels[:, None], axis=0)
    outgoing = jnp.take(tiles, inverse, axis=1)
    received = lax.all_to_all(outgoing, ("gx", "gy"), split_axis=1, concat_axis=1, tiled=True)
    return (adjoint_field, received[None])


def solution(mesh):
    placed = (
        P("gx", "gy", None),
        P("gx", "gy", None),
        P(None, "gx", "gy", None),
        P(None, "gx", "gy", None),
        P("gx", "gy", None),
        P(("gx", "gy"), None),
        P(("gx", "gy"), None),
        P(("gx", "gy")),
        P(("gx", "gy")),
        P(("gx", "gy"), None),
    )
    return jax.shard_map(
        body,
        mesh=mesh,
        in_specs=placed,
        out_specs=(P("gx", "gy", None), P(("gx", "gy"), None, None, None)),
        check_vma=False,
    )
```

profile of v0, /device:TPU:0, one launch (start us, length us, event | category | flops | bytes accessed | tf_op | source)
XLA Modules:
  0.0 257.6 jit_solution(10952993467441159841)
XLA Ops:
  0.7 1.8 pad_maximum_fusion.5
  2.5 4.9 %collective-permute-start = (f32[4,1,32,256]{3,2,1,0:T(8,128)}, f32[4,1,32,256]{3,2,1,0:T(8,128)S(1)}, u32[]{:S(2)}, u32[]{:S(2)}) collective-permute-start(f32[4,1,32,256]{3,2,1,0:T(8,128)} %get-tuple-element.21), channel_id=1, source_target_pairs={{0,8},{8,16},{16,24},{1,9},{9,17},{17,25},{2,10},{10,18},{18,26},{... | collective-permute-start | bytes 393224 | tf_op jit(solution)/shard_map/ppermute | solution.py:17
  7.4 1.3 collective-permute-start.1
  10.3 1.6 scatter_custom_fusion
  12.6 7.1 %all-to-all-start = ((s32[32,1,9]{2,1,0:T(1,128)}), s32[32,1,9]{2,1,0:T(1,128)}, u32[]{:S(2)}, u32[]{:S(2)}) async-start(s32[32,1,9]{2,1,0:T(1,128)} %bitcast.8), calls=%async_computation | async-start | bytes 32768 | tf_op jit(solution)/shard_map/all_to_all | solution.py:112
  19.8 2.0 pad_maximum_fusion.3
  21.9 2.7 %collective-permute-start.2 = (f32[4,34,1,256]{3,2,1,0:T(1,128)}, f32[4,34,1,256]{3,2,1,0:T(1,128)}, u32[]{:S(2)}, u32[]{:S(2)}) collective-permute-start(f32[4,34,1,256]{3,2,1,0:T(1,128)} %get-tuple-element.19), channel_id=1, source_target_pairs={{0,1},{1,2},{2,3},{3,4},{4,5},{5,6},{6,7},{8,9},{9,10},{10,11},{11... | collective-permute-start | bytes 417800 | tf_op jit(solution)/shard_map/ppermute | solution.py:17
  26.4 1.5 scatter_custom_fusion.1
  28.6 2.3 reshape.107
  30.9 7.5 %all-to-all-start.1 = ((f32[32,9,128]{2,1,0:T(8,128)}), f32[32,9,128]{2,1,0:T(8,128)}, u32[]{:S(2)}, u32[]{:S(2)}) async-start(f32[32,9,128]{2,1,0:T(8,128)} %reshape.110), calls=%async_computation.1 | async-start | bytes 524288 | tf_op jit(solution)/shard_map/all_to_all | solution.py:105
  38.9 1.4 reduce.7
  40.5 6.6 %select_maximum_fusion = f32[3,34,34,258]{3,2,1,0:T(8,128)S(1)} fusion(f32[4,34,1,256]{3,2,1,0:T(1,128)} %collective-permute-done.3, f32[4,34,1,256]{3,2,1,0:T(1,128)} %collective-permute-done.2, f32[4,1,32,256]{3,2,1,0:T(8,128)S(1)} %collective-permute-done.1, f32[4,1,32,256]{3,2,1,0:T(8,128)S(1)} %collective-permute-done, ...), kind=kLoop, calls=%fused_computation.6 | loop fusion | flops 12526416 | bytes 8313952 | tf_op jit(solution)/shard_map/concatenate | solution.py:21
  47.0 2.9 %add_multiply_fusion = (f32[34,34,258]{2,1,0:T(8,128)}, f32[34,34,258]{2,1,0:T(8,128)S(1)}, f32[34,34,258]{2,1,0:T(8,128)}, f32[34,34,258]{2,1,0:T(8,128)}) fusion(f32[3,34,34,258]{3,2,1,0:T(8,128)S(1)} %select_maximum_fusion), kind=kLoop, calls=%fused_computation.52 | loop fusion | flops 2385984 | bytes 8350944 | tf_op jit(solution)/shard_map/div | solution.py:43
  49.9 3.3 %slice_bitcast_fusion = (f32[34,34,258]{2,1,0:T(8,128)}, f32[34,34,258]{2,1,0:T(8,128)}, f32[34,34,258]{2,1,0:T(8,128)}) fusion(f32[3,34,34,258]{3,2,1,0:T(8,128)S(1)} %select_maximum_fusion), kind=kLoop, calls=%fused_computation.49 | loop fusion | bytes 7157952 | tf_op jit(solution)/shard_map/squeeze | solution.py:44
  55.4 1.6 reshape.142
  57.0 4.5 %scatter_fusion = f32[2048,128]{1,0:T(8,128)} fusion(f32[2048,128]{1,0:T(8,128)} %reshape.107, s32[288]{0:T(512)S(1)} %fusion.184, f32[288,128]{1,0:T(8,128)} %reshape.142), kind=kCustom, calls=%fused_computation.3 | custom fusion | flops 36864 | bytes 443520 | tf_op jit(solution)/shard_map/scatter-add | solution.py:123
  61.5 2.5 reshape.112
  64.0 24.5 %fusion.175 = f32[1,32,32,256]{3,2,1,0:T(8,128)S(1)} fusion(f32[32,32,256]{2,1,0:T(8,128)} %reshape.112, f32[34,34,256]{2,1,0:T(8,128)S(1)} %maximum_bitcast_fusion, f32[34,34,258]{2,1,0:T(8,128)S(1)} %get-tuple-element.16, f32[34,34,258]{2,1,0:T(8,128)} %get-tuple-element.18, f32[34,34,258]{2,1,0:T(8,128)} %get-tuple-element.17, ...), kind=kLoop, calls=%fused_computation.275 | loop fusion | flops 41943040 | bytes 47529984 | tf_op jit(solution)/shard_map/broadcast_in_dim | solution.py:129
  88.6 3.7 %collective-permute-start.4 = (f32[1,1,32,256]{3,2,1,0:T(8,128)S(1)}, f32[1,1,32,256]{3,2,1,0:T(8,128)S(1)}, u32[]{:S(2)}, u32[]{:S(2)}) collective-permute-start(f32[1,1,32,256]{3,2,1,0:T(8,128)S(1)} %get-tuple-element.25), channel_id=1, source_target_pairs={{0,8},{8,16},{16,24},{1,9},{9,17},{17,25},{2,10},{10,18},{18,26},{... | collective-permute-start | bytes 98312 | tf_op jit(solution)/shard_map/ppermute | solution.py:17
  92.3 1.3 collective-permute-start.5
  93.9 4.2 %collective-permute-done.5 = f32[1,1,32,256]{3,2,1,0:T(8,128)S(1)} collective-permute-done((f32[1,1,32,256]{3,2,1,0:T(8,128)S(1)}, f32[1,1,32,256]{3,2,1,0:T(8,128)S(1)}, u32[]{:S(2)}, u32[]{:S(2)}) %collective-permute-start.5) | collective-permute-done | bytes 32800 | tf_op jit(solution)/shard_map/ppermute | solution.py:20
  98.2 1.3 collective-permute-start.6
  100.8 3.5 %collective-permute-done.7 = f32[1,34,1,256]{3,2,1,0:T(1,128)S(1)} collective-permute-done((f32[1,34,1,256]{3,2,1,0:T(1,128)S(1)}, f32[1,34,1,256]{3,2,1,0:T(1,128)S(1)}, u32[]{:S(2)}, u32[]{:S(2)}) %collective-permute-start.7) | collective-permute-done | bytes 34848 | tf_op jit(solution)/shard_map/ppermute | solution.py:20
  104.3 1.4 maximum_bitcast_fusion.1
  105.7 25.7 %fusion.188 = (f32[32,32,256]{2,1,0:T(8,128)}, f32[32,32,256]{2,1,0:T(8,128)}) fusion(f32[32,32,256]{2,1,0:T(8,128)} %param.14, f32[32,32,256]{2,1,0:T(8,128)S(1)} %copy-done.4, f32[34,34,258]{2,1,0:T(8,128)S(1)} %get-tuple-element.16, f32[34,34,256]{2,1,0:T(8,128)S(1)} %maximum_bitcast_fusion.1, f32[34,34,258]{2,1,0:T(8,128)} %get-tuple-element.18, ...), kind=kLoop, calls=%fused_computation.314 | loop fusion | flops 42205184 | bytes 49627136 | tf_op jit(solution)/shard_map/sub | solution.py:131
  131.3 2.6 %broadcast_multiply_fusion = f32[3,32,32,256]{3,2,1,0:T(8,128)S(1)} fusion(f32[3,32,32,256]{3,2,1,0:T(8,128)} %param.13, f32[32,32,256]{2,1,0:T(8,128)} %get-tuple-element.10), kind=kLoop, calls=%fused_computation.55 | loop fusion | flops 786432 | bytes 7340032 | tf_op jit(solution)/shard_map/mul | solution.py:131
  133.9 2.3 reshape.113
  136.3 6.0 %copy.24 = f32[3,32,8192]{2,0,1:T(4,128)} copy(f32[3,32,8192]{2,1,0:T(8,128)} %reshape.113) | data formatting | bytes 6291456 | tf_op jit(solution)/shard_map/reshape | solution.py:133
  142.3 6.9 %gather_fusion = f32[32,3,8192]{2,1,0:T(4,128)} fusion(f32[3,32,8192]{2,0,1:T(4,128)} %copy.24, s32[1024]{0:T(1024)S(1)} %pad_clamp_fusion), kind=kCustom, calls=%fused_computation | custom fusion | bytes 6291584 | tf_op jit(solution)/shard_map/jit(_take)/gather | solution.py:136
  149.2 3.3 %select_bitcast_fusion = f32[3,32,8192]{2,0,1:T(4,128)S(1)} fusion(f32[32,3,8192]{2,1,0:T(4,128)} %gather_fusion, pred[32]{0:T(512)(128)(4,1)S(1)} %compare_and_fusion), kind=kLoop, calls=%fused_computation.48 | loop fusion | flops 786432 | bytes 6291488 | tf_op jit(solution)/shard_map/jit(_take)/select_n | solution.py:136
  152.6 101.6 %all_to_all.19 = f32[3,32,8192]{2,0,1:T(4,128)S(1)} all-to-all(f32[3,32,8192]{2,0,1:T(4,128)S(1)} %select_bitcast_fusion), channel_id=1, replica_groups=mesh['gx'=4,'gy'=8] {'gx','gy'}, dimensions={1} | all-to-all | bytes 6291456 | tf_op jit(solution)/shard_map/all_to_all | solution.py:137
  254.1 3.5 %copy.25 = f32[1,3,32,8192]{3,2,1,0:T(8,128)} copy(f32[1,3,32,8192]{3,1,2,0:T(4,128)S(1)} %bitcast.69) | data formatting | bytes 6291456
  (61 shorter events, 8.7 us)
Async XLA Ops:
  0.6 8.7 %copy-start.9 = (s32[256,1]{0,1:T(1,128)S(1)}, s32[256,1]{0,1:T(1,128)}, u32[]{:S(2)}) copy-start(s32[256,1]{0,1:T(1,128)} %param.16) | copy-start | bytes 3076
  0.6 19.1 %copy-start.12 = (s32[1,32]{1,0:T(1,128)S(1)}, s32[1,32]{1,0:T(1,128)}, u32[]{:S(2)}) copy-start(s32[1,32]{1,0:T(1,128)} %param.19) | copy-start | bytes 388
  0.6 19.2 %copy-start = (f32[3,32,32,256]{3,2,1,0:T(8,128)S(1)}, f32[3,32,32,256]{3,2,1,0:T(8,128)}, u32[]{:S(2)}) copy-start(f32[3,32,32,256]{3,2,1,0:T(8,128)} %param.12) | copy-start | bytes 9437188
  2.5 17.3 %collective-permute-start = (f32[4,1,32,256]{3,2,1,0:T(8,128)}, f32[4,1,32,256]{3,2,1,0:T(8,128)S(1)}, u32[]{:S(2)}, u32[]{:S(2)}) collective-permute-start(f32[4,1,32,256]{3,2,1,0:T(8,128)} %get-tuple-element.21), channel_id=1, source_target_pairs={{0,8},{8,16},{16,24},{1,9},{9,17},{17,25},{2,10},{10,18},{18,26},{... | collective-permute-start | bytes 393224 | tf_op jit(solution)/shard_map/ppermute | solution.py:17
  7.4 12.5 %collective-permute-start.1 = (f32[4,1,32,256]{3,2,1,0:T(8,128)}, f32[4,1,32,256]{3,2,1,0:T(8,128)S(1)}, u32[]{:S(2)}, u32[]{:S(2)}) collective-permute-start(f32[4,1,32,256]{3,2,1,0:T(8,128)} %get-tuple-element.22), channel_id=1, source_target_pairs={{8,0},{16,8},{24,16},{9,1},{17,9},{25,17},{10,2},{18,10},{26,18},{... | collective-permute-start | bytes 393224 | tf_op jit(solution)/shard_map/ppermute | solution.py:20
  10.3 11.6 %copy-start.10 = (s32[256,1]{0,1:T(1,128)}, s32[256,1]{0,1:T(1,128)S(1)}, u32[]{:S(2)}) copy-start(s32[256,1]{0,1:T(1,128)S(1)} %compare_select_fusion.1) | copy-start | bytes 3076
  12.6 18.4 %all-to-all-start = ((s32[32,1,9]{2,1,0:T(1,128)}), s32[32,1,9]{2,1,0:T(1,128)}, u32[]{:S(2)}, u32[]{:S(2)}) async-start(s32[32,1,9]{2,1,0:T(1,128)} %bitcast.8), calls=%async_computation | async-start | bytes 32768 | tf_op jit(solution)/shard_map/all_to_all | solution.py:112
  19.8 6.1 %copy-start.13 = (s32[32]{0:T(128)}, s32[32]{0:T(128)S(1)}, u32[]{:S(2)}) copy-start(s32[32]{0:T(128)S(1)} %select_reduce_fusion) | copy-start | bytes 388
  19.8 20.6 %copy-start.5 = (f32[4,1,32,256]{3,2,1,0:T(8,128)}, f32[4,1,32,256]{3,2,1,0:T(8,128)S(1)}, u32[]{:S(2)}) copy-start(f32[4,1,32,256]{3,2,1,0:T(8,128)S(1)} %collective-permute-done) | copy-start | bytes 393220
  19.8 20.6 %copy-start.7 = (f32[4,1,32,256]{3,2,1,0:T(8,128)}, f32[4,1,32,256]{3,2,1,0:T(8,128)S(1)}, u32[]{:S(2)}) copy-start(f32[4,1,32,256]{3,2,1,0:T(8,128)S(1)} %collective-permute-done.1) | copy-start | bytes 393220
  21.9 18.6 %collective-permute-start.2 = (f32[4,34,1,256]{3,2,1,0:T(1,128)}, f32[4,34,1,256]{3,2,1,0:T(1,128)}, u32[]{:S(2)}, u32[]{:S(2)}) collective-permute-start(f32[4,34,1,256]{3,2,1,0:T(1,128)} %get-tuple-element.19), channel_id=1, source_target_pairs={{0,1},{1,2},{2,3},{3,4},{4,5},{5,6},{6,7},{8,9},{9,10},{10,11},{11... | collective-permute-start | bytes 417800 | tf_op jit(solution)/shard_map/ppermute | solution.py:17
  24.6 15.9 %collective-permute-start.3 = (f32[4,34,1,256]{3,2,1,0:T(1,128)}, f32[4,34,1,256]{3,2,1,0:T(1,128)}, u32[]{:S(2)}, u32[]{:S(2)}) collective-permute-start(f32[4,34,1,256]{3,2,1,0:T(1,128)} %get-tuple-element.20), channel_id=1, source_target_pairs={{1,0},{2,1},{3,2},{4,3},{5,4},{6,5},{7,6},{9,8},{10,9},{11,10},{12... | collective-permute-start | bytes 417800 | tf_op jit(solution)/shard_map/ppermute | solution.py:20
  30.9 24.5 %all-to-all-start.1 = ((f32[32,9,128]{2,1,0:T(8,128)}), f32[32,9,128]{2,1,0:T(8,128)}, u32[]{:S(2)}, u32[]{:S(2)}) async-start(f32[32,9,128]{2,1,0:T(8,128)} %reshape.110), calls=%async_computation.1 | async-start | bytes 524288 | tf_op jit(solution)/shard_map/all_to_all | solution.py:105
  49.9 3.8 %copy-start.1 = (f32[3,32,32,256]{3,2,1,0:T(8,128)S(1)}, f32[3,32,32,256]{3,2,1,0:T(8,128)}, u32[]{:S(2)}) copy-start(f32[3,32,32,256]{3,2,1,0:T(8,128)} %param.12) | copy-start | bytes 9437188
  49.9 4.4 %copy-start.2 = (f32[32,32,256]{2,1,0:T(8,128)S(1)}, f32[32,32,256]{2,1,0:T(8,128)}, u32[]{:S(2)}) copy-start(f32[32,32,256]{2,1,0:T(8,128)} %param.10) | copy-start | bytes 3145732
  49.9 4.4 %copy-start.6 = (f32[4,1,32,256]{3,2,1,0:T(8,128)S(1)}, f32[4,1,32,256]{3,2,1,0:T(8,128)}, u32[]{:S(2)}) copy-start(f32[4,1,32,256]{3,2,1,0:T(8,128)} %copy-done.5) | copy-start | bytes 393220
  49.9 4.5 %copy-start.8 = (f32[4,1,32,256]{3,2,1,0:T(8,128)S(1)}, f32[4,1,32,256]{3,2,1,0:T(8,128)}, u32[]{:S(2)}) copy-start(f32[4,1,32,256]{3,2,1,0:T(8,128)} %copy-done.7) | copy-start | bytes 393220
  64.0 29.6 %copy-start.14 = (s32[32]{0:T(128)S(1)}, s32[32]{0:T(128)}, u32[]{:S(2)}) copy-start(s32[32]{0:T(128)} %copy-done.13) | copy-start | bytes 388
  64.0 36.8 %copy-start.11 = (s32[32]{0:T(128)S(1)}, s32[32]{0:T(128)}, u32[]{:S(2)}) copy-start(s32[32]{0:T(128)} %fusion.187) | copy-start | bytes 388
  88.5 12.3 %copy-start.3 = (f32[1,32,32,256]{3,2,1,0:T(8,128)}, f32[1,32,32,256]{3,2,1,0:T(8,128)S(1)}, u32[]{:S(2)}) copy-start(f32[1,32,32,256]{3,2,1,0:T(8,128)S(1)} %fusion.175) | copy-start | bytes 3145732
  88.5 17.1 %copy-start.4 = (f32[32,32,256]{2,1,0:T(8,128)S(1)}, f32[32,32,256]{2,1,0:T(8,128)}, u32[]{:S(2)}) copy-start(f32[32,32,256]{2,1,0:T(8,128)} %reshape.112) | copy-start | bytes 3145732
  88.6 5.3 %collective-permute-start.4 = (f32[1,1,32,256]{3,2,1,0:T(8,128)S(1)}, f32[1,1,32,256]{3,2,1,0:T(8,128)S(1)}, u32[]{:S(2)}, u32[]{:S(2)}) collective-permute-start(f32[1,1,32,256]{3,2,1,0:T(8,128)S(1)} %get-tuple-element.25), channel_id=1, source_target_pairs={{0,8},{8,16},{16,24},{1,9},{9,17},{17,25},{2,10},{10,18},{18,26},{... | collective-permute-start | bytes 98312 | tf_op jit(solution)/shard_map/ppermute | solution.py:17
  92.3 5.8 %collective-permute-start.5 = (f32[1,1,32,256]{3,2,1,0:T(8,128)S(1)}, f32[1,1,32,256]{3,2,1,0:T(8,128)S(1)}, u32[]{:S(2)}, u32[]{:S(2)}) collective-permute-start(f32[1,1,32,256]{3,2,1,0:T(8,128)S(1)} %get-tuple-element.26), channel_id=1, source_target_pairs={{8,0},{16,8},{24,16},{9,1},{17,9},{25,17},{10,2},{18,10},{26,18},{... | collective-permute-start | bytes 98312 | tf_op jit(solution)/shard_map/ppermute | solution.py:20
  98.2 2.6 %collective-permute-start.6 = (f32[1,34,1,256]{3,2,1,0:T(1,128)S(1)}, f32[1,34,1,256]{3,2,1,0:T(1,128)S(1)}, u32[]{:S(2)}, u32[]{:S(2)}) collective-permute-start(f32[1,34,1,256]{3,2,1,0:T(1,128)S(1)} %get-tuple-element.23), channel_id=1, source_target_pairs={{0,1},{1,2},{2,3},{3,4},{4,5},{5,6},{6,7},{8,9},{9,10},{10,11},{11... | collective-permute-start | bytes 104456 | tf_op jit(solution)/shard_map/ppermute | solution.py:17
  99.5 4.8 %collective-permute-start.7 = (f32[1,34,1,256]{3,2,1,0:T(1,128)S(1)}, f32[1,34,1,256]{3,2,1,0:T(1,128)S(1)}, u32[]{:S(2)}, u32[]{:S(2)}) collective-permute-start(f32[1,34,1,256]{3,2,1,0:T(1,128)S(1)} %get-tuple-element.24), channel_id=1, source_target_pairs={{1,0},{2,1},{3,2},{4,3},{5,4},{6,5},{7,6},{9,8},{10,9},{11,10},{12... | collective-permute-start | bytes 104456 | tf_op jit(solution)/shard_map/ppermute | solution.py:20
where the time goes:
time: 259 us; the launch traced here: 258 us
  blocking collectives  102 us (39%)
  other arithmetic  79 us (31%)
  local copies, waits for them, and re-layouts  35 us (14%)
  starting transfers between devices  32.3 us (12%)
  waiting for transfers between devices  7.96 us (3%)
    all_to_all x1, blocking collectives, body(): lax.all_to_all(outgoing, ('gx', 'gy'), split_axis=1, concat_axis=1, tiled...  102 us
    sub x1, other arithmetic, body(): thermal_load = expansion * (adjoint_field - ref_temp)[None]  25.7 us
    broadcast_in_dim x1, other arithmetic, body(): first_pad = exchange_rim(first[None], 1)[0]  24.5 us
    ppermute x4, starting transfers between devices, padded_2(): lax.ppermute(lax.slice_in_dim(block, block.shape[dim] - width, None, axis...  12.6 us
    reshape x2, local copies, waits for them, and re-layouts, body(): tiles = thermal_load.reshape(3, devices, tile_cells)  8.33 us
    ppermute x4, waiting for transfers between devices, padded_2(): lax.ppermute(lax.slice_in_dim(block, 0, width, axis=dim), axis, backward)  7.7 us
    all_to_all x1, starting transfers between devices, body(): lax.all_to_all(send_rows.reshape(devices, capacity, row_width), ('gx', 'g...  7.45 us
    all_to_all x1, starting transfers between devices, body(): lax.all_to_all(send_lines.reshape(devices, capacity), ('gx', 'gy'), split...  7.13 us
  transfers between devices with their start and end apart: 10, of which 3 were waited for; matrix products, arithmetic and copies ran while one was open for 10% of the time, Pallas kernels for 0%

commit v1 on v0

v1 whole, which is shorter than its diff:
```python
import jax
import jax.numpy as jnp
from jax import lax
from jax.experimental import pallas as pl
from jax.experimental.pallas import tpu as pltpu
from jax.sharding import PartitionSpec as P

OMEGA = 0.8
W1, W2, W3 = 1.0, 0.25, 0.125
C2 = W2 / 2.0
C3 = W3 / 3.0
CENTRE = 2.0 * W1 + 4.0 * W2 + 8.0 * W3 / 3.0
MIB = 1 << 20
LANES = 128
F32 = jnp.float32
BF16 = jnp.bfloat16
VMEM = pltpu.MemorySpace.VMEM
SMEM = pltpu.MemorySpace.SMEM


def whole(count, space=VMEM):
    return [pl.BlockSpec(memory_space=space) for _ in range(count)]


def call(kernel, outs, scratch=(), specs=None, limit=24, name=None):
    return pl.pallas_call(
        kernel,
        out_shape=outs,
        in_specs=specs,
        out_specs=jax.tree.map(lambda _: pl.BlockSpec(memory_space=VMEM), outs),
        scratch_shapes=list(scratch),
        compiler_params=pltpu.CompilerParams(vmem_limit_bytes=limit * MIB),
        name=name,
    )


def shape(*dims):
    return jax.ShapeDtypeStruct(dims, F32)


def parts_of(value, count):
    parts = []
    for _ in range(count):
        part = value.astype(BF16)
        parts.append(part)
        value = value - part.astype(F32)
    return parts


def dot(left, right, **kw):
    return jnp.dot(left, right, preferred_element_type=F32, **kw)


def pack_kernel(count_ref, rows_ref, dest_ref, line_ref, out_ref, *, devices, capacity, pitch):
    rows_dev = rows_ref.shape[0]
    dest = dest_ref[...]
    line = line_ref[...]
    live = lax.broadcasted_iota(jnp.int32, (1, rows_dev), 1) < count_ref[0]
    brick = lax.broadcasted_iota(jnp.int32, (devices, rows_dev), 0)
    named = jnp.where((brick == dest) & live, 1.0, 0.0)
    before = lax.broadcasted_iota(jnp.int32, (rows_dev, rows_dev), 0)
    after = lax.broadcasted_iota(jnp.int32, (rows_dev, rows_dev), 1)
    earlier = dot(named.astype(BF16), jnp.where(before < after, 1.0, 0.0).astype(BF16))
    slot = jnp.sum(named * earlier, axis=0, keepdims=True).astype(jnp.int32)
    target = jnp.where(live, dest * pitch + slot, -1)
    place = lax.broadcasted_iota(jnp.int32, (devices * pitch, rows_dev), 0)
    chosen = jnp.where(place == target, 1.0, 0.0).astype(BF16)
    width = rows_ref.shape[1]
    placed = dot(chosen, jnp.concatenate(parts_of(rows_ref[...], 3), axis=1))
    out_ref[...] = placed[:, :width] + (placed[:, width : 2 * width] + placed[:, 2 * width :])
    column = lax.broadcasted_iota(jnp.int32, (width, rows_dev), 0)
    here = jnp.where((column == slot) & live, (line + 1).astype(F32), 0.0)
    lines = lax.dot_general(
        named,
        here,
        (((1,), (1,)), ((), ())),
        precision=lax.Precision.HIGHEST,
        preferred_element_type=F32,
    )
    out_ref[pl.ds(capacity, devices, stride=pitch), :] = lines


def along_z(value):
    lanes = value.shape[1]
    lane = lax.broadcasted_iota(jnp.int32, value.shape, 1)
    low = jnp.where(lane == 0, 0.0, pltpu.roll(value, 1, 1))
    high = jnp.where(lane == lanes - 1, 0.0, pltpu.roll(value, lanes - 1, 1))
    return low + high


def along_y(value):
    rows = value.shape[0]
    return pltpu.roll(value, 1, 0)[: rows - 8] + pltpu.roll(value, rows - 1, 0)[: rows - 8]


def set_rim(rim_ref, f, low, high, pad_x):
    for piece in range(rim_ref.shape[1]):
        lanes = slice(piece * LANES, (piece + 1) * LANES)
        rim_ref[f, piece, pl.ds(0, pad_x, stride=8), :] = high[:, lanes]
        rim_ref[f, piece, pl.ds(7, pad_x, stride=8), :] = low[:, lanes]


def with_rim(rim_ref, f, value, x):
    rim = [rim_ref[f, piece, pl.ds(x * 8, 8), :] for piece in range(rim_ref.shape[1])]
    return jnp.concatenate([value, jnp.concatenate(rim, axis=1)], axis=0)


def product_terms(a, b, c):
    size_y = a.shape[0] - 8
    ya, yb, yc = along_y(a), along_y(b), along_y(c)
    a, c = a[:size_y], c[:size_y]
    flat = yb + along_z(c + C2 * (yb + yc))
    side = a + C2 * (ya + yb) + along_z(C2 * (a + c) + C3 * (ya + yb + yc))
    return flat, side


def field_terms(v):
    size_y = v.shape[0] - 8
    u = along_z(v)
    yv, yu = along_y(v), along_y(u)
    v, u = v[:size_y], u[:size_y]
    ex = v + C2 * (u + yv) + C3 * yu
    ey = C2 * yv + C3 * yu
    ez = C2 * u + C3 * yu
    gy = yv + C2 * yu
    gz = u + C2 * yu
    return ex, ey, ez, gy, gz


def sweep_one_kernel(
    temp_ref, cond_ref, load_ref, xlo_ref, xhi_ref, ylo_ref, yhi_ref,
    base_ref, rate_ref, source_ref, rim_ref,
    ex_ref, ey_ref, ez_ref, sv_ref, sk_ref, pv_ref, pk_ref,
    *, size_x, size_y, pad_x,
):
    for f in range(4):
        set_rim(rim_ref, f, ylo_ref[f], yhi_ref[f], pad_x)

    def terms(values, x):
        tiles = [with_rim(rim_ref, f, values[f], x) for f in range(4)]
        v, kx, ky, kz = tiles
        ex, ey, ez, gy, gz = field_terms(v)
        flat_v, side_v = product_terms(kx * v, ky * v, kz * v)
        flat_k, side_k = product_terms(kx, ky, kz)
        ex_ref[x], ey_ref[x], ez_ref[x] = ex, ey, ez
        sv_ref[x], sk_ref[x] = side_v, side_k
        return ky[:size_y] * gy + kz[:size_y] * gz + flat_v, flat_k

    terms([xlo_ref[f] for f in range(4)], 0)
    terms([xhi_ref[f] for f in range(4)], size_x + 1)

    def first_pass(x, carry):
        at = pl.ds(pl.multiple_of(x * size_y, size_y), size_y)
        values = [temp_ref[at, :]] + [cond_ref[f, at, :] for f in range(3)]
        pv_ref[x], pk_ref[x] = terms(values, x + 1)
        return carry

    lax.fori_loop(0, size_x, first_pass, 0)

    def second_pass(x, carry):
        at = pl.ds(pl.multiple_of(x * size_y, size_y), size_y)
        kx, ky, kz = [cond_ref[f, at, :] for f in range(3)]
        h = (
            pv_ref[x]
            + kx * (ex_ref[x] + ex_ref[x + 2])
            + ky * (ey_ref[x] + ey_ref[x + 2])
            + kz * (ez_ref[x] + ez_ref[x + 2])
            + (sv_ref[x] + sv_ref[x + 2])
        )
        d = 1.0 + 0.5 * (CENTRE * (kx + ky + kz) + pk_ref[x] + (sk_ref[x] + sk_ref[x + 2]))
        rate = OMEGA / d
        load = rate * load_ref[at, :]
        rate_ref[at, :] = rate
        source_ref[at, :] = load
        base_ref[at, :] = (1.0 - OMEGA) * temp_ref[at, :] + load + (0.5 * rate) * h
        return carry

    lax.fori_loop(0, size_x, second_pass, 0)


def wall_kernel(
    got_ref, base_ref, rate_ref, source_ref,
    first_ref, total_ref, xrim_ref, yrim_ref, split_ref,
    *, devices, capacity, pitch, size_x, size_y, step,
):
    slots = devices * pitch
    width = got_ref.shape[1]
    lines = got_ref[pl.ds(capacity, devices, stride=pitch), :]
    slot = lax.broadcasted_iota(jnp.int32, (width, slots), 0)
    entry = lax.broadcasted_iota(jnp.int32, (width, slots), 1) % pitch
    spread = dot(
        lines,
        jnp.where((slot == entry) & (slot < capacity), 1.0, 0.0),
        precision=lax.Precision.HIGHEST,
    )
    holder = lax.broadcasted_iota(jnp.int32, (devices, slots), 0)
    own = lax.broadcasted_iota(jnp.int32, (devices, slots), 1) // pitch
    line = jnp.sum(jnp.where(holder == own, spread, 0.0), axis=0, keepdims=True).astype(jnp.int32) - 1
    parts = jnp.concatenate(parts_of(got_ref[...], 3), axis=1)
    lanes = base_ref.shape[1]
    pieces = lanes // width

    def block(i, carry):
        at = pl.ds(pl.multiple_of(i * step, step), step)
        cell = lax.broadcasted_iota(jnp.int32, (step, slots), 0) + i * step
        walls = []
        for piece in range(pieces):
            chosen = jnp.where(cell * pieces + piece == line, 1.0, 0.0).astype(BF16)
            wall = dot(chosen, parts)
            walls.append(wall[:, :width] + (wall[:, width : 2 * width] + wall[:, 2 * width :]))
        added = rate_ref[at, :] * jnp.concatenate(walls, axis=1)
        first = base_ref[at, :] + added
        first_ref[at, :] = first
        for piece in range(pieces):
            split_ref[piece, at, :] = first[:, piece * width : (piece + 1) * width]
        total_ref[at, :] = source_ref[at, :] + added
        return carry

    lax.fori_loop(0, base_ref.shape[0] // step, block, 0)
    xrim_ref[0] = first_ref[pl.ds(0, size_y), :]
    xrim_ref[1] = first_ref[pl.ds((size_x - 1) * size_y, size_y), :]
    for piece in range(pieces):
        at = slice(piece * width, (piece + 1) * width)
        yrim_ref[0, :, at] = split_ref[piece, pl.ds(0, size_x, stride=size_y), :]
        yrim_ref[1, :, at] = split_ref[piece, pl.ds(size_y - 1, size_x, stride=size_y), :]


def sweep_two_kernel(
    owner_ref, first_ref, cond_ref, rate_ref, total_ref, reft_ref, expand_ref,
    xlo_ref, xhi_ref, ylo_ref, yhi_ref, fxlo_ref, fxhi_ref, fylo_ref, fyhi_ref,
    field_ref, late_ref,
    rim_ref, ex_ref, ey_ref, ez_ref, sv_ref, pv_ref,
    *, size_x, size_y, pad_x, tile_rows,
):
    set_rim(rim_ref, 0, fylo_ref[0], fyhi_ref[0], pad_x)
    for f in range(1, 4):
        set_rim(rim_ref, f, ylo_ref[f], yhi_ref[f], pad_x)

    def terms(values, x):
        tiles = [with_rim(rim_ref, f, values[f], x) for f in range(4)]
        v, kx, ky, kz = tiles
        ex, ey, ez, gy, gz = field_terms(v)
        flat_v, side_v = product_terms(kx * v, ky * v, kz * v)
        ex_ref[x], ey_ref[x], ez_ref[x] = ex, ey, ez
        sv_ref[x] = side_v
        return ky[:size_y] * gy + kz[:size_y] * gz + flat_v

    terms([fxlo_ref[0]] + [xlo_ref[f] for f in range(1, 4)], 0)
    terms([fxhi_ref[0]] + [xhi_ref[f] for f in range(1, 4)], size_x + 1)

    def first_pass(x, carry):
        at = pl.ds(pl.multiple_of(x * size_y, size_y), size_y)
        values = [first_ref[at, :]] + [cond_ref[f, at, :] for f in range(3)]
        pv_ref[x] = terms(values, x + 1)
        return carry

    lax.fori_loop(0, size_x, first_pass, 0)
    per_plane = size_y // tile_rows

    def second_pass(x, carry):
        at = pl.ds(pl.multiple_of(x * size_y, size_y), size_y)
        kx, ky, kz = [cond_ref[f, at, :] for f in range(3)]
        h = (
            pv_ref[x]
            + kx * (ex_ref[x] + ex_ref[x + 2])
            + ky * (ey_ref[x] + ey_ref[x + 2])
            + kz * (ez_ref[x] + ez_ref[x + 2])
            + (sv_ref[x] + sv_ref[x + 2])
        )
        field = (1.0 - OMEGA) * first_ref[at, :] + total_ref[at, :] + (0.5 * rate_ref[at, :]) * h
        field_ref[at, :] = field
        strain = field - reft_ref[at, :]
        for part in range(per_plane):
            owner = owner_ref[0, x * per_plane + part]
            rows = slice(part * tile_rows, (part + 1) * tile_rows)
            for c in range(3):
                load = (expand_ref[c, at, :] * strain)[rows]
                for piece in range(late_ref.shape[2]):
                    late_ref[owner, c, piece] = load[:, piece * LANES : (piece + 1) * LANES]
        return carry

    lax.fori_loop(0, size_x, second_pass, 0)


def settle_kernel(late_ref, out_ref, *, tile_rows, pieces):
    c, block = pl.program_id(0), pl.program_id(1)
    pitch = 3 * pieces * tile_rows
    for y in range(tile_rows):
        for piece in range(pieces):
            start = block * 8 * pitch + (c * pieces + piece) * tile_rows + y
            lane = (y * pieces + piece) * LANES
            out_ref[0, 0, :, lane : lane + LANES] = late_ref[pl.ds(start, 8, stride=pitch), :]


def neighbours(axis):
    count = lax.axis_size(axis)
    up = [(i, i + 1) for i in range(count - 1)]
    return up, [(b, a) for a, b in up]


def body(
    adjoint_temp, adjoint_load, conductivity, expansion, ref_temp,
    wall_rows, wall_dest, wall_line, wall_count, tile_owner,
):
    axes = ("gx", "gy")
    devices = lax.axis_size("gx") * lax.axis_size("gy")
    size_x, size_y, size_z = adjoint_temp.shape
    rows_dev, width = wall_rows.shape
    cells = size_x * size_y
    capacity = (rows_dev + devices - 1) // devices + 1
    pitch = (capacity + 1 + 7) // 8 * 8
    pad_x = size_x + 8
    tile_rows = cells // devices
    up_x, down_x = neighbours("gx")
    up_y, down_y = neighbours("gy")

    packed = call(
        lambda *refs: pack_kernel(*refs, devices=devices, capacity=capacity, pitch=pitch),
        shape(devices * pitch, width),
        specs=whole(1, SMEM) + whole(3),
        name="pack_rows",
    )(wall_count, wall_rows, wall_dest.reshape(1, rows_dev), wall_line.reshape(1, rows_dev))
    got = lax.all_to_all(
        packed.reshape(devices, pitch, width), axes, split_axis=0, concat_axis=0, tiled=True
    ).reshape(devices * pitch, width)

    stacked = lambda at: jnp.concatenate([adjoint_temp[at][None], conductivity[:, at]], axis=0)
    xlo = lax.ppermute(stacked(size_x - 1), "gx", up_x)
    xhi = lax.ppermute(stacked(0), "gx", down_x)

    def edge(at):
        lines = jnp.concatenate([adjoint_temp[None, :, at], conductivity[:, :, at]], axis=0)
        return jnp.concatenate(
            [xlo[:, None, at], lines, xhi[:, None, at], jnp.zeros((4, pad_x - size_x - 2, size_z), F32)],
            axis=1,
        )

    ylo = lax.ppermute(edge(size_y - 1), "gy", up_y)
    yhi = lax.ppermute(edge(0), "gy", down_y)

    flat = lambda array: array.reshape(array.shape[:-3] + (cells, size_z))
    temp, cond, load = flat(adjoint_temp), flat(conductivity), flat(adjoint_load)
    plane = pltpu.VMEM((size_x, size_y, size_z), F32)
    wide = pltpu.VMEM((size_x + 2, size_y, size_z), F32)
    pieces = size_z // LANES
    rims = pltpu.VMEM((4, pieces, pad_x * 8, LANES), F32)
    grid = shape(cells, size_z)
    base, rate, source = call(
        lambda *refs: sweep_one_kernel(*refs, size_x=size_x, size_y=size_y, pad_x=pad_x),
        (grid, grid, grid),
        scratch=[rims] + [wide] * 5 + [plane] * 2,
        specs=whole(7),
        limit=40,
        name="sweep_one",
    )(temp, cond, load, xlo, xhi, ylo, yhi)
    first, total, xrim, yrim = call(
        lambda *refs: wall_kernel(
            *refs, devices=devices, capacity=capacity, pitch=pitch,
            size_x=size_x, size_y=size_y, step=cells // 8,
        ),
        (grid, grid, shape(2, size_y, size_z), shape(2, size_x, size_z)),
        scratch=[pltpu.VMEM((pieces, cells, LANES), F32)],
        specs=whole(4),
        name="wall_source",
    )(got, base, rate, source)

    fxlo = lax.ppermute(xrim[1:2], "gx", up_x)
    fxhi = lax.ppermute(xrim[0:1], "gx", down_x)

    def rim_edge(side, at):
        return jnp.concatenate(
            [fxlo[:, at : at + 1], yrim[side : side + 1], fxhi[:, at : at + 1],
             jnp.zeros((1, pad_x - size_x - 2, size_z), F32)],
            axis=1,
        )

    fylo = lax.ppermute(rim_edge(1, size_y - 1), "gy", up_y)
    fyhi = lax.ppermute(rim_edge(0, 0), "gy", down_y)

    field, late = call(
        lambda *refs: sweep_two_kernel(
            *refs, size_x=size_x, size_y=size_y, pad_x=pad_x, tile_rows=tile_rows
        ),
        (grid, shape(devices, 3, pieces, tile_rows, LANES)),
        scratch=[rims] + [wide] * 4 + [plane],
        specs=whole(1, SMEM) + whole(14),
        limit=40,
        name="sweep_two",
    )(tile_owner, first, cond, rate, total, flat(ref_temp), flat(expansion),
      xlo, xhi, ylo, yhi, fxlo, fxhi, fylo, fyhi)

    moved = lax.all_to_all(late, axes, split_axis=0, concat_axis=0, tiled=True)
    tile_cells = tile_rows * size_z
    block_load = pl.pallas_call(
        lambda *refs: settle_kernel(*refs, tile_rows=tile_rows, pieces=pieces),
        out_shape=shape(1, 3, devices, tile_cells),
        grid=(3, devices // 8),
        in_specs=whole(1),
        out_specs=pl.BlockSpec((1, 1, 8, tile_cells), lambda c, b: (0, c, b, 0)),
        compiler_params=pltpu.CompilerParams(vmem_limit_bytes=16 * MIB),
        name="settle",
    )(moved.reshape(devices * 3 * pieces * tile_rows, LANES))
    return field.reshape(size_x, size_y, size_z), block_load


def solution(mesh):
    placed = (
        P("gx", "gy", None),
        P("gx", "gy", None),
        P(None, "gx", "gy", None),
        P(None, "gx", "gy", None),
        P("gx", "gy", None),
        P(("gx", "gy"), None),
        P(("gx", "gy"), None),
        P(("gx", "gy")),
        P(("gx", "gy")),
        P(("gx", "gy"), None),
    )
    return jax.shard_map(
        body,
        mesh=mesh,
        in_specs=placed,
        out_specs=(P("gx", "gy", None), P(("gx", "gy"), None, None, None)),
        check_vma=False,
    )
```

time: 259 us -> 165 us (0.64)
  other arithmetic: 79 us -> 1.5 us
  Pallas kernels: 0 us -> 24.6 us
  blocking collectives: 102 us -> 84.2 us
  local copies, waits for them, and re-layouts: 35 us -> 20 us
  waiting for transfers between devices: 7.96 us -> 3.39 us
  starting transfers between devices: 32.3 us -> 29.4 us
    sub x1 -> x0, other arithmetic: 25.7 us -> none  [body(): thermal_load = expansion * (adjoint_field - ref_temp)[None]]
    pallas_call x0 -> x5, Pallas kernels: none -> 24.6 us  [the longest x1 7.57 us: body(): call(lambda *refs: sweep_one_kernel(*refs, size_x=size_x, size_y=size_y,...]
    broadcast_in_dim x1 -> x0, other arithmetic: 24.5 us -> none  [body(): first_pad = exchange_rim(first[None], 1)[0]]
    all_to_all x1, blocking collectives: 102 us -> 84.2 us  [body(): moved = lax.all_to_all(late, axes, split_axis=0, concat_axis=0, tiled=True)]
    reshape x7 -> x0, local copies, waits for them, and re-layouts: 15.5 us -> none  [the longest x2 8.33 us: body(): tiles = thermal_load.reshape(3, devices, tile_cells)]
    unnamed x31 -> x40, local copies, waits for them, and re-layouts: 4.67 us -> 14.6 us
    gather x1 -> x0, local copies, waits for them, and re-layouts: 6.95 us -> none  [body(): outgoing = jnp.take(tiles, inverse, axis=1)]
    all_to_all x2 -> x1, starting transfers between devices: 14.6 us -> 7.65 us  [body(): lax.all_to_all(packed.reshape(devices, pitch, width), axes, split_axis=0,...]
  transfers between devices with their start and end apart: 10 -> 9, of which waited for: 3 -> 3; matrix products, arithmetic and copies ran while one was open for 10% -> 3% of each run, Pallas kernels for 0% -> 5%
where the time goes in v1:
time: 165 us
  blocking collectives  84.2 us (51%)
  starting transfers between devices  29.4 us (18%)
  Pallas kernels  24.6 us (15%)
  local copies, waits for them, and re-layouts  20 us (12%)
  waiting for transfers between devices  3.39 us (2%)
    all_to_all x1, blocking collectives, body(): moved = lax.all_to_all(late, axes, split_axis=0, concat_axis=0, tiled=True)  84.2 us
    unnamed x40, local copies, waits for them, and re-layouts  14.6 us
    all_to_all x1, starting transfers between devices, body(): lax.all_to_all(packed.reshape(devices, pitch, width), axes, split_axis=0,...  7.65 us
    pallas_call x1, Pallas kernels, body(): call(lambda *refs: sweep_one_kernel(*refs, size_x=size_x, size_y=size_y,...  7.57 us
    pallas_call x1, Pallas kernels, body(): call(lambda *refs: sweep_two_kernel(*refs, size_x=size_x, size_y=size_y,...  7.41 us
    pallas_call x1, Pallas kernels, body(): pl.pallas_call(lambda *refs: settle_kernel(*refs, tile_rows=tile_rows, pi...  5.31 us
    ppermute x1, starting transfers between devices, body(): xlo = lax.ppermute(stacked(size_x - 1), 'gx', up_x)  4.87 us
    ppermute x1, starting transfers between devices, body(): fxlo = lax.ppermute(xrim[1:2], 'gx', up_x)  4.55 us
  transfers between devices with their start and end apart: 9, of which 3 were waited for; matrix products, arithmetic and copies ran while one was open for 3% of the time, Pallas kernels for 5%

profile of v1, /device:TPU:0, one launch (start us, length us, event | category | flops | bytes accessed | tf_op | source)
XLA Modules:
  0.0 164.6 jit_solution(16653997878171421346)
XLA Ops:
  0.6 0.9 fusion.2
  1.6 1.0 slice_bitcast_fusion
  3.2 4.9 %collective-permute-start = (f32[4,32,256]{2,1,0:T(8,128)}, f32[4,32,256]{2,1,0:T(8,128)S(1)}, u32[]{:S(2)}, u32[]{:S(2)}) collective-permute-start(f32[4,32,256]{2,1,0:T(8,128)} %pad_maximum_fusion), channel_id=1, source_target_pairs={{0,8},{8,16},{16,24},{1,9},{9,17},{17,25},{2,10},{10,18},{18,26},{... | collective-permute-start | bytes 393224 | tf_op jit(solution)/shard_map/ppermute | solution.py:328
  8.8 1.3 collective-permute-start.1
  10.7 0.9 copy-done.16
  13.0 1.3 pack_rows.1
  14.3 7.7 %all-to-all-start = ((f32[32,16,128]{2,1,0:T(8,128)}), f32[32,16,128]{2,1,0:T(8,128)S(1)}, u32[]{:S(2)}, u32[]{:S(2)}) async-start(f32[32,16,128]{2,1,0:T(8,128)} %bitcast.2), calls=%async_computation | async-start | bytes 524288 | tf_op jit(solution)/shard_map/all_to_all | solution.py:323
  21.9 1.1 fusion.1
  23.0 1.5 fusion
  25.6 1.3 collective-permute-start.3
  26.9 3.0 %collective-permute-start.2 = (f32[4,40,256]{2,1,0:T(8,128)S(1)}, f32[4,40,256]{2,1,0:T(8,128)S(1)}, u32[]{:S(2)}, u32[]{:S(2)}) collective-permute-start(f32[4,40,256]{2,1,0:T(8,128)S(1)} %get-tuple-element.43), channel_id=1, source_target_pairs={{0,1},{1,2},{2,3},{3,4},{4,5},{5,6},{6,7},{8,9},{9,10},{10,11},{11... | collective-permute-start | bytes 491528 | tf_op jit(solution)/shard_map/ppermute | solution.py:338
  29.9 1.0 collective-permute-done.2.refs_5_.refs_9_
  30.9 1.2 copy-done.5
  32.2 1.2 copy-done.10
  33.4 7.6 %sweep_one.1 = (f32[1024,256]{1,0:T(8,128)S(1)}, f32[1024,256]{1,0:T(8,128)S(1)}, f32[1024,256]{1,0:T(8,128)S(1)}) custom-call(f32[1024,256]{1,0:T(8,128)S(1)} %bitcast.31, f32[3,1024,256]{2,1,0:T(8,128)S(1)} %bitcast.27, f32[1024,256]{1,0:T(8,128)S(1)} %bitcast.32, f32[4,32,256]{2,1,0:T(8,128)S(1)} %collective-permute-done.refs_3_.refs_7_, ...), custom_call_target="tpu_custom_call" | custom-call | tf_op jit(solution)/shard_map/sweep_one/pallas_call | solution.py:348
  41.0 1.0 copy-done.1
  41.9 1.0 copy-done.6
  42.9 1.0 copy-done.8
  45.3 1.2 copy-done.2
  46.5 1.2 copy-done.7
  47.7 1.2 copy-done.9
  49.0 3.0 %wall_source.1 = (f32[1024,256]{1,0:T(8,128)S(1)}, f32[1024,256]{1,0:T(8,128)S(1)}, f32[2,32,256]{2,1,0:T(8,128)S(1)}, f32[2,32,256]{2,1,0:T(8,128)S(1)}) custom-call(f32[512,128]{1,0:T(8,128)S(1)} %bitcast.33, f32[1024,256]{1,0:T(8,128)S(1)} %copy-done.7, f32[1024,256]{1,0:T(8,128)S(1)} %copy-done.2, f32[1024,256]{1,0:T(8,128)S(1)} %copy-done.9), custom_call_target="tpu_custom_call" | custom-call | tf_op jit(solution)/shard_map/wall_source/pallas_call | solution.py:356
  52.0 1.3 collective-permute-start.5
  53.3 4.5 %collective-permute-start.4 = (f32[1,32,256]{2,1,0:T(8,128)S(1)}, f32[1,32,256]{2,1,0:T(8,128)S(1)}, u32[]{:S(2)}, u32[]{:S(2)}) collective-permute-start(f32[1,32,256]{2,1,0:T(8,128)S(1)} %get-tuple-element.35), channel_id=1, source_target_pairs={{0,8},{8,16},{16,24},{1,9},{9,17},{17,25},{2,10},{10,18},{18,26},{... | collective-permute-start | bytes 98312 | tf_op jit(solution)/shard_map/ppermute | solution.py:367
  57.9 1.5 collective-permute-done.4.refs_11_
  59.5 1.3 collective-permute-start.7
  60.8 4.1 %collective-permute-start.6 = (f32[1,40,256]{2,1,0:T(8,128)S(1)}, f32[1,40,256]{2,1,0:T(8,128)S(1)}, u32[]{:S(2)}, u32[]{:S(2)}) collective-permute-start(f32[1,40,256]{2,1,0:T(8,128)S(1)} %get-tuple-element.41), channel_id=1, source_target_pairs={{0,1},{1,2},{2,3},{3,4},{4,5},{5,6},{6,7},{8,9},{9,10},{10,11},{11... | collective-permute-start | bytes 122888 | tf_op jit(solution)/shard_map/ppermute | solution.py:377
  64.9 0.8 collective-permute-done.6.refs_13_
  65.8 1.9 %copy-done.4 = f32[3,32,32,256]{3,2,1,0:T(8,128)S(1)} copy-done((f32[3,32,32,256]{3,2,1,0:T(8,128)S(1)}, f32[3,32,32,256]{3,2,1,0:T(8,128)}, u32[]{:S(2)}) %copy-start.4) | copy-done | bytes 3145752
  67.7 7.4 %sweep_two.1 = (f32[1024,256]{1,0:T(8,128)}, f32[32,3,2,32,128]{4,3,2,1,0:T(8,128)S(1)}) custom-call(s32[1,32]{1,0:T(1,128)S(1)} %copy-done.19, f32[1024,256]{1,0:T(8,128)S(1)} %get-tuple-element.14.refs_1_, f32[3,1024,256]{2,1,0:T(8,128)S(1)} %bitcast.28, f32[1024,256]{1,0:T(8,128)S(1)} %copy-done.3, f32[1024,256]{1,0:T(8,128)S(1)} %get-tuple-element.15.refs_4_, ...), custom_call_target="tpu_custom_call" | custom-call | tf_op jit(solution)/shard_map/sweep_two/pallas_call | solution.py:380
  75.1 84.2 %all_to_all.10 = f32[32,3,2,32,128]{4,3,2,1,0:T(8,128)S(1)} all-to-all(f32[32,3,2,32,128]{4,3,2,1,0:T(8,128)S(1)} %get-tuple-element.19), channel_id=1, replica_groups=mesh['gx'=4,'gy'=8] {'gx','gy'}, dimensions={0} | all-to-all | bytes 6291456 | tf_op jit(solution)/shard_map/all_to_all | solution.py:392
  159.2 5.3 %settle.1 = f32[1,3,32,8192]{3,2,1,0:T(8,128)} custom-call(f32[6144,128]{1,0:T(8,128)S(1)} %bitcast.29), custom_call_target="tpu_custom_call" | custom-call | tf_op jit(solution)/shard_map/settle/pallas_call | solution.py:394
  (50 shorter events, 5.2 us)
Async XLA Ops:
  0.6 30.3 %copy-start = (f32[3,32,32,256]{3,2,1,0:T(8,128)S(1)}, f32[3,32,32,256]{3,2,1,0:T(8,128)}, u32[]{:S(2)}) copy-start(f32[3,32,32,256]{3,2,1,0:T(8,128)} %param.12) | copy-start | bytes 9437188
  3.2 21.4 %collective-permute-start = (f32[4,32,256]{2,1,0:T(8,128)}, f32[4,32,256]{2,1,0:T(8,128)S(1)}, u32[]{:S(2)}, u32[]{:S(2)}) collective-permute-start(f32[4,32,256]{2,1,0:T(8,128)} %pad_maximum_fusion), channel_id=1, source_target_pairs={{0,8},{8,16},{16,24},{1,9},{9,17},{17,25},{2,10},{10,18},{18,26},{... | collective-permute-start | bytes 393224 | tf_op jit(solution)/shard_map/ppermute | solution.py:328
  8.8 15.9 %collective-permute-start.1 = (f32[4,32,256]{2,1,0:T(8,128)}, f32[4,32,256]{2,1,0:T(8,128)}, u32[]{:S(2)}, u32[]{:S(2)}) collective-permute-start(f32[4,32,256]{2,1,0:T(8,128)} %pad_maximum_fusion.1), channel_id=1, source_target_pairs={{8,0},{16,8},{24,16},{9,1},{17,9},{25,17},{10,2},{18,10},{26,18},{... | collective-permute-start | bytes 393224 | tf_op jit(solution)/shard_map/ppermute | solution.py:329
  10.7 0.9 copy-start.16
  11.6 0.7 copy-start.17
  12.3 0.7 copy-start.18
  14.3 31.0 %all-to-all-start = ((f32[32,16,128]{2,1,0:T(8,128)}), f32[32,16,128]{2,1,0:T(8,128)S(1)}, u32[]{:S(2)}, u32[]{:S(2)}) async-start(f32[32,16,128]{2,1,0:T(8,128)} %bitcast.2), calls=%async_computation | async-start | bytes 524288 | tf_op jit(solution)/shard_map/all_to_all | solution.py:323
  25.6 4.4 %collective-permute-start.3 = (f32[4,40,256]{2,1,0:T(8,128)S(1)}, f32[4,40,256]{2,1,0:T(8,128)S(1)}, u32[]{:S(2)}, u32[]{:S(2)}) collective-permute-start(f32[4,40,256]{2,1,0:T(8,128)S(1)} %get-tuple-element.42), channel_id=1, source_target_pairs={{1,0},{2,1},{3,2},{4,3},{5,4},{6,5},{7,6},{9,8},{10,9},{11,10},{12... | collective-permute-start | bytes 491528 | tf_op jit(solution)/shard_map/ppermute | solution.py:339
  26.9 4.0 %collective-permute-start.2 = (f32[4,40,256]{2,1,0:T(8,128)S(1)}, f32[4,40,256]{2,1,0:T(8,128)S(1)}, u32[]{:S(2)}, u32[]{:S(2)}) collective-permute-start(f32[4,40,256]{2,1,0:T(8,128)S(1)} %get-tuple-element.43), channel_id=1, source_target_pairs={{0,1},{1,2},{2,3},{3,4},{4,5},{5,6},{6,7},{8,9},{9,10},{10,11},{11... | collective-permute-start | bytes 491528 | tf_op jit(solution)/shard_map/ppermute | solution.py:338
  30.9 1.2 copy-start.5
  32.2 1.2 copy-start.10
  41.0 1.0 copy-start.1
  41.9 1.0 copy-start.6
  42.9 1.0 copy-start.8
  43.9 0.7 copy-start.12
  44.6 0.7 copy-start.14
  45.3 20.5 %copy-start.19 = (s32[1,32]{1,0:T(1,128)S(1)}, s32[1,32]{1,0:T(1,128)}, u32[]{:S(2)}) copy-start(s32[1,32]{1,0:T(1,128)} %refs_0_.2) | copy-start | bytes 388
  45.3 1.2 copy-start.2
  46.5 1.2 copy-start.7
  47.7 1.2 copy-start.9
  49.0 16.8 %copy-start.3 = (f32[1024,256]{1,0:T(8,128)S(1)}, f32[1024,256]{1,0:T(8,128)}, u32[]{:S(2)}) copy-start(f32[1024,256]{1,0:T(8,128)} %copy-done.1) | copy-start | bytes 3145732
  49.0 16.8 %copy-start.11 = (f32[32,32,256]{2,1,0:T(8,128)S(1)}, f32[32,32,256]{2,1,0:T(8,128)}, u32[]{:S(2)}) copy-start(f32[32,32,256]{2,1,0:T(8,128)} %param.14) | copy-start | bytes 3145732
  49.0 16.8 %copy-start.13 = (f32[4,40,256]{2,1,0:T(8,128)S(1)}, f32[4,40,256]{2,1,0:T(8,128)}, u32[]{:S(2)}) copy-start(f32[4,40,256]{2,1,0:T(8,128)} %copy-done.12) | copy-start | bytes 491524
  49.0 16.8 %copy-start.15 = (f32[4,40,256]{2,1,0:T(8,128)S(1)}, f32[4,40,256]{2,1,0:T(8,128)}, u32[]{:S(2)}) copy-start(f32[4,40,256]{2,1,0:T(8,128)} %copy-done.14) | copy-start | bytes 491524
  52.0 5.9 %collective-permute-start.5 = (f32[1,32,256]{2,1,0:T(8,128)S(1)}, f32[1,32,256]{2,1,0:T(8,128)S(1)}, u32[]{:S(2)}, u32[]{:S(2)}) collective-permute-start(f32[1,32,256]{2,1,0:T(8,128)S(1)} %get-tuple-element.34), channel_id=1, source_target_pairs={{8,0},{16,8},{24,16},{9,1},{17,9},{25,17},{10,2},{18,10},{26,18},{... | collective-permute-start | bytes 98312 | tf_op jit(solution)/shard_map/ppermute | solution.py:368
  53.3 6.1 %collective-permute-start.4 = (f32[1,32,256]{2,1,0:T(8,128)S(1)}, f32[1,32,256]{2,1,0:T(8,128)S(1)}, u32[]{:S(2)}, u32[]{:S(2)}) collective-permute-start(f32[1,32,256]{2,1,0:T(8,128)S(1)} %get-tuple-element.35), channel_id=1, source_target_pairs={{0,8},{8,16},{16,24},{1,9},{9,17},{17,25},{2,10},{10,18},{18,26},{... | collective-permute-start | bytes 98312 | tf_op jit(solution)/shard_map/ppermute | solution.py:367
  59.5 5.4 %collective-permute-start.7 = (f32[1,40,256]{2,1,0:T(8,128)S(1)}, f32[1,40,256]{2,1,0:T(8,128)S(1)}, u32[]{:S(2)}, u32[]{:S(2)}) collective-permute-start(f32[1,40,256]{2,1,0:T(8,128)S(1)} %get-tuple-element.40), channel_id=1, source_target_pairs={{1,0},{2,1},{3,2},{4,3},{5,4},{6,5},{7,6},{9,8},{10,9},{11,10},{12... | collective-permute-start | bytes 122888 | tf_op jit(solution)/shard_map/ppermute | solution.py:378
  60.8 5.0 %collective-permute-start.6 = (f32[1,40,256]{2,1,0:T(8,128)S(1)}, f32[1,40,256]{2,1,0:T(8,128)S(1)}, u32[]{:S(2)}, u32[]{:S(2)}) collective-permute-start(f32[1,40,256]{2,1,0:T(8,128)S(1)} %get-tuple-element.41), channel_id=1, source_target_pairs={{0,1},{1,2},{2,3},{3,4},{4,5},{5,6},{6,7},{8,9},{9,10},{10,11},{11... | collective-permute-start | bytes 122888 | tf_op jit(solution)/shard_map/ppermute | solution.py:377
  65.8 1.9 %copy-start.4 = (f32[3,32,32,256]{3,2,1,0:T(8,128)S(1)}, f32[3,32,32,256]{3,2,1,0:T(8,128)}, u32[]{:S(2)}) copy-start(f32[3,32,32,256]{3,2,1,0:T(8,128)} %param.13) | copy-start | bytes 9437188

commit v2 on v1

v2 whole, which is shorter than its diff:
```python
import jax
import jax.numpy as jnp
from jax import lax
from jax.experimental import pallas as pl
from jax.experimental.pallas import tpu as pltpu
from jax.sharding import PartitionSpec as P


OMEGA = 0.8
W1, W2, W3 = 1.0, 0.25, 0.125
C2 = W2 / 2.0
C3 = W3 / 3.0
CENTRE = 2.0 * W1 + 4.0 * W2 + 8.0 * W3 / 3.0
MIB = 1 << 20
LANES = 128
CORNER_ROWS = 3
EARLY_EIGHTHS = 2
GROUPS = 4
AXES = ("gx", "gy")
F32 = jnp.float32
BF16 = jnp.bfloat16
VMEM = pltpu.MemorySpace.VMEM
SMEM = pltpu.MemorySpace.SMEM
HBM = pltpu.MemorySpace.HBM


def whole(count, space=VMEM):
    return [pl.BlockSpec(memory_space=space) for _ in range(count)]


def call(kernel, outs, scratch=(), specs=None, limit=60):
    return pl.pallas_call(
        kernel,
        out_shape=outs,
        in_specs=specs,
        out_specs=jax.tree.map(lambda _: pl.BlockSpec(memory_space=HBM), outs),
        scratch_shapes=list(scratch),
        compiler_params=pltpu.CompilerParams(vmem_limit_bytes=limit * MIB),
    )


def shape(*dims):
    return jax.ShapeDtypeStruct(dims, F32)


def parts_of(value, count):
    parts = []
    for _ in range(count):
        part = value.astype(BF16)
        parts.append(part)
        value = value - part.astype(F32)
    return parts


def dot(left, right, **kw):
    return jnp.dot(left, right, preferred_element_type=F32, **kw)


def lanes_of(piece):
    return slice(piece * LANES, (piece + 1) * LANES)


def split(value):
    return [value[:, lanes_of(p)] for p in range(value.shape[1] // LANES)]


def diagonal(move_x, move_y):
    count_x, count_y = lax.axis_size("gx"), lax.axis_size("gy")
    at_x, at_y = lax.axis_index("gx") + move_x, lax.axis_index("gy") + move_y
    there = (at_x >= 0) & (at_x < count_x) & (at_y >= 0) & (at_y < count_y)
    return jnp.where(there, at_x * count_y + at_y, 0), there


CORNERS = [(-1, -1), (-1, 1), (1, -1), (1, 1)]


def fetch(pairs, sems, start=0):
    copies = [pltpu.make_async_copy(src, dst, sems.at[start + i]) for i, (src, dst) in enumerate(pairs)]
    for copy in copies:
        copy.start()
    return copies


def wait(copies):
    for copy in copies:
        copy.wait()


def prepare_kernel(
    count_ref, rows_hbm, dest_hbm, line_hbm, temp_hbm, cond_hbm,
    packed_hbm, below_hbm, above_hbm, low_hbm, high_hbm,
    rows_ref, dest_ref, line_ref, outer_ref, sides_ref, out_ref, low_ref, high_ref, sems,
    *, devices, capacity, pitch, size_x, size_y,
):
    fields = [temp_hbm] + [cond_hbm.at[f] for f in range(3)]
    small = fetch([(rows_hbm, rows_ref), (dest_hbm, dest_ref), (line_hbm, line_ref)], sems)
    wanted = []
    for f, field in enumerate(fields):
        for side, x in enumerate((0, size_x - 1)):
            wanted.append((field.at[x], outer_ref.at[side, f]))
        for side, y in enumerate((0, size_y - 8)):
            wanted.append((field.at[:, pl.ds(y, 8), :], sides_ref.at[side, f]))
    large = fetch(wanted, sems, 3)
    wait(small)

    rows_dev, width = rows_ref.shape
    dest = dest_ref[...]
    line = line_ref[...]
    live = lax.broadcasted_iota(jnp.int32, (1, rows_dev), 1) < count_ref[0]
    brick = lax.broadcasted_iota(jnp.int32, (devices, rows_dev), 0)
    named = jnp.where((brick == dest) & live, 1.0, 0.0)
    before = lax.broadcasted_iota(jnp.int32, (rows_dev, rows_dev), 0)
    after = lax.broadcasted_iota(jnp.int32, (rows_dev, rows_dev), 1)
    earlier = dot(named.astype(BF16), jnp.where(before < after, 1.0, 0.0).astype(BF16))
    slot = jnp.sum(named * earlier, axis=0, keepdims=True).astype(jnp.int32)
    target = jnp.where(live, dest * pitch + slot, -1)
    place = lax.broadcasted_iota(jnp.int32, (devices * pitch, rows_dev), 0)
    chosen = jnp.where(place == target, 1.0, 0.0).astype(BF16)
    placed = dot(chosen, jnp.concatenate(parts_of(rows_ref[...], 3), axis=1))
    out_ref[...] = placed[:, :width] + (placed[:, width : 2 * width] + placed[:, 2 * width :])
    column = lax.broadcasted_iota(jnp.int32, (width, rows_dev), 0)
    here = jnp.where((column == slot) & live, (line + 1).astype(F32), 0.0)
    lines = lax.dot_general(
        named,
        here,
        (((1,), (1,)), ((), ())),
        precision=lax.Precision.HIGHEST,
        preferred_element_type=F32,
    )
    out_ref[pl.ds(capacity, devices, stride=pitch), :] = lines

    wait(large)
    for move_x, move_y in CORNERS:
        brick, there = diagonal(move_x, move_y)
        side, row = (0 if move_x < 0 else 1), (0 if move_y < 0 else size_y - 1)
        v, kx, ky, kz = [outer_ref[side, f, row : row + 1, :] for f in range(4)]

        @pl.when(there)
        def _():
            row = brick * pitch + capacity + 1
            for value in (v, kx + ky, kz):
                for part in split(value):
                    out_ref[pl.ds(row, 1), :] = part
                    row = row + 1

    sent = fetch([(out_ref, packed_hbm), (outer_ref.at[0], below_hbm), (outer_ref.at[1], above_hbm)], sems)
    for f in range(4):
        for x in range(size_x):
            low_ref[f, x : x + 1, :] = sides_ref[0, f, x, 0:1, :]
            high_ref[f, x : x + 1, :] = sides_ref[1, f, x, 7:8, :]
    wait(sent + fetch([(low_ref, low_hbm), (high_ref, high_hbm)], sems, 3))


def along_z(pieces):
    lane = lax.broadcasted_iota(jnp.int32, pieces[0].shape, 1)
    up = [pltpu.roll(p, 1, 1) for p in pieces]
    down = [pltpu.roll(p, LANES - 1, 1) for p in pieces]
    last = len(pieces) - 1
    return [
        jnp.where(lane == 0, up[i - 1] if i > 0 else 0.0, up[i])
        + jnp.where(lane == LANES - 1, down[i + 1] if i < last else 0.0, down[i])
        for i in range(last + 1)
    ]


def along_y(pieces):
    rows = pieces[0].shape[0]
    return [pltpu.roll(p, 1, 0)[: rows - 8] + pltpu.roll(p, rows - 1, 0)[: rows - 8] for p in pieces]


def each(function, *lists):
    return [function(*values) for values in zip(*lists)]


def inner(pieces):
    return [p[: p.shape[0] - 8] for p in pieces]


def product_terms(a, b, c, side_only=False):
    ya, yb, yc = along_y(a), along_y(b), along_y(c)
    a, c = inner(a), inner(c)
    yab = each(lambda s, t: s + t, ya, yb)
    side_z = along_z(each(lambda a, c, yab, yc: C2 * (a + c) + C3 * (yab + yc), a, c, yab, yc))
    side = each(lambda a, yab, z: a + C2 * yab + z, a, yab, side_z)
    if side_only:
        return None, side
    flat_z = along_z(each(lambda c, yb, yc: c + C2 * (yb + yc), c, yb, yc))
    return each(lambda yb, z: yb + z, yb, flat_z), side


def field_terms(v):
    u = along_z(v)
    yv, yu = along_y(v), along_y(u)
    v, u = inner(v), inner(u)
    c3yu = each(lambda yu: C3 * yu, yu)
    ey = each(lambda yv, t: C2 * yv + t, yv, c3yu)
    c2u = each(lambda u: C2 * u, u)
    ez = each(lambda s, t: s + t, c2u, c3yu)
    ex = each(lambda v, s, t: v + s + t, v, c2u, ey)
    c2yu = each(lambda yu: C2 * yu, yu)
    gy = each(lambda yv, t: yv + t, yv, c2yu)
    gz = each(lambda u, t: u + t, u, c2yu)
    return ex, ey, ez, gy, gz


def put(ref, x, pieces):
    for p, value in enumerate(pieces):
        ref[x, :, lanes_of(p)] = value


def set_rim(rim_ref, f, low, high, size_x):
    for p in range(rim_ref.shape[1]):
        rim_ref[f, p, pl.ds(8, size_x, stride=8), :] = high[:, lanes_of(p)]
        rim_ref[f, p, pl.ds(15, size_x, stride=8), :] = low[:, lanes_of(p)]


def with_rim(rim_ref, f, value, x):
    return [
        jnp.concatenate([piece, rim_ref[f, p, pl.ds(x * 8, 8), :]], axis=0)
        for p, piece in enumerate(split(value))
    ]


def plane_terms(tiles, x, terms_refs, side_only=False):
    v, kx, ky, kz = tiles
    ex, ey, ez, gy, gz = field_terms(v)
    times = lambda k: each(lambda k, v: k * v, k, v)
    flat, side = product_terms(times(kx), times(ky), times(kz), side_only)
    for ref, value in zip(terms_refs, (ex, ey, ez, side)):
        put(ref, x, value)
    if side_only:
        return None
    return each(lambda ky, gy, kz, gz, f: ky * gy + kz * gz + f, inner(ky), gy, inner(kz), gz, flat)


def coupled(k, partial, before, after):
    both = [low[...] + high[...] for low, high in zip(before, after)]
    return partial + k[0] * both[0] + k[1] * both[1] + k[2] * both[2] + both[3]


def first_kernel(
    temp_hbm, cond_hbm, load_hbm, xlo_hbm, xhi_hbm, ylo_hbm, yhi_hbm, got_hbm,
    first_hbm, total_hbm, rate_hbm, krim_hbm, low_hbm, high_hbm,
    temp_ref, cond_ref, load_ref, first_ref, total_ref, rate_ref, rim_ref, low_ref, high_ref,
    ex_ref, ey_ref, ez_ref, sv_ref, sk_ref, pv_ref, pk_ref,
    outer_ref, ylo_ref, yhi_ref, got_ref, parts_ref, split_ref, sems,
    *, devices, size_x, size_y, capacity, pitch, step, groups,
):
    copies = fetch(
        [(ylo_hbm, ylo_ref), (yhi_hbm, yhi_ref), (got_hbm, got_ref),
         (xlo_hbm, outer_ref.at[0]), (xhi_hbm, outer_ref.at[1])], sems,
    )
    rows = first_ref.shape[0] // groups
    part = lambda g: pl.ds(g * rows, rows)
    loads = [
        fetch([(temp_hbm.at[part(g)], temp_ref.at[part(g)]), (cond_hbm.at[:, part(g)], cond_ref.at[:, part(g)])],
              sems, 5 + 2 * g)
        for g in range(groups)
    ]
    load = fetch([(load_hbm, load_ref)], sems, 5 + 2 * groups)
    wait(copies)
    pieces = rim_ref.shape[1]
    for f in range(4):
        set_rim(rim_ref, f, ylo_ref[f], yhi_ref[f], size_x)
    for move_x, move_y in CORNERS:
        brick, there = diagonal(move_x, move_y)
        row = brick * pitch + capacity + 1
        at = (0 if move_x < 0 else size_x + 1) * 8 + (7 if move_y < 0 else 0)
        for p in range(pieces):
            for i, f in enumerate((0, 1, 3)):
                value = got_ref[pl.ds(row + i * pieces + p, 1), :]
                rim_ref[f, p, at : at + 1, :] = jnp.where(there, value, 0.0)
            rim_ref[2, p, at : at + 1, :] = jnp.zeros((1, LANES), F32)
    sent = fetch([(rim_ref, krim_hbm)], sems)

    def terms(values, x, side_only=False):
        tiles = [with_rim(rim_ref, f, values[f], x) for f in range(4)]
        partial = plane_terms(tiles, x, (ex_ref, ey_ref, ez_ref, sv_ref), side_only)
        flat, side = product_terms(*tiles[1:], side_only)
        put(sk_ref, x, side)
        return partial, flat

    terms([outer_ref[0, f] for f in range(4)], 0, True)
    terms([outer_ref[1, f] for f in range(4)], size_x + 1, True)

    def first_pass(x, carry):
        at = pl.ds(pl.multiple_of(x * size_y, size_y), size_y)
        values = [temp_ref[at, :]] + [cond_ref[f, at, :] for f in range(3)]
        partial, flat = terms(values, x + 1)
        put(pv_ref, x, partial)
        put(pk_ref, x, flat)
        return carry

    each_group = size_x // groups
    for g in range(groups):
        wait(loads[g])
        lax.fori_loop(g * each_group, (g + 1) * each_group, first_pass, 0)
    wait(load)

    def second_pass(x, carry):
        at = pl.ds(pl.multiple_of(x * size_y, size_y), size_y)
        k = [cond_ref[f, at, :] for f in range(3)]
        refs = (ex_ref, ey_ref, ez_ref, sv_ref)
        h = coupled(k, pv_ref[x], [r.at[x] for r in refs], [r.at[x + 2] for r in refs])
        d = 1.0 + 0.5 * (CENTRE * (k[0] + k[1] + k[2]) + pk_ref[x] + (sk_ref[x] + sk_ref[x + 2]))
        rate = OMEGA / d
        load = rate * load_ref[at, :]
        rate_ref[at, :] = rate
        total_ref[at, :] = load
        first_ref[at, :] = (1.0 - OMEGA) * temp_ref[at, :] + load + (0.5 * rate) * h
        return carry

    lax.fori_loop(0, size_x, second_pass, 0)

    slots = devices * pitch
    width = got_ref.shape[1]
    lines = got_ref[pl.ds(capacity, devices, stride=pitch), :]
    slot = lax.broadcasted_iota(jnp.int32, (width, slots), 0)
    entry = lax.broadcasted_iota(jnp.int32, (width, slots), 1) % pitch
    spread = dot(
        lines,
        jnp.where((slot == entry) & (slot < capacity), 1.0, 0.0),
        precision=lax.Precision.HIGHEST,
    )
    holder = lax.broadcasted_iota(jnp.int32, (devices, slots), 0)
    own = lax.broadcasted_iota(jnp.int32, (devices, slots), 1) // pitch
    line = jnp.sum(jnp.where(holder == own, spread, 0.0), axis=0, keepdims=True).astype(jnp.int32) - 1
    parts_ref[...] = jnp.concatenate(parts_of(got_ref[...], 2), axis=1)

    def block(i, carry):
        at = pl.ds(pl.multiple_of(i * step, step), step)
        cell = lax.broadcasted_iota(jnp.int32, (step, slots), 0) + i * step
        for piece in range(pieces):
            chosen = jnp.where(cell * pieces + piece == line, 1.0, 0.0).astype(BF16)
            wall = dot(chosen, parts_ref[...])
            lanes = lanes_of(piece)
            added = rate_ref[at, lanes] * (wall[:, :width] + wall[:, width:])
            first = first_ref[at, lanes] + added
            first_ref[at, lanes] = first
            split_ref[piece, at, :] = first
            total_ref[at, lanes] = total_ref[at, lanes] + added
        return carry

    steps = first_ref.shape[0] // step // groups
    for g in range(groups):
        lax.fori_loop(g * steps, (g + 1) * steps, block, 0)
        sent += fetch(
            [(ref.at[part(g)], hbm.at[part(g)])
             for ref, hbm in ((first_ref, first_hbm), (total_ref, total_hbm), (rate_ref, rate_hbm))],
            sems, 1 + 3 * g,
        )
    for piece in range(pieces):
        low_ref[:, lanes_of(piece)] = split_ref[piece, pl.ds(0, size_x, stride=size_y), :]
        high_ref[:, lanes_of(piece)] = split_ref[piece, pl.ds(size_y - 1, size_x, stride=size_y), :]
    wait(sent + fetch([(low_ref, low_hbm), (high_ref, high_hbm)], sems, 1 + 3 * groups))


def planes_kernel(first_hbm, ylo_hbm, yhi_hbm, below_hbm, above_hbm, ylo_ref, yhi_ref, send_ref, sems, *, size_x, size_y):
    copies = fetch([(ylo_hbm, ylo_ref), (yhi_hbm, yhi_ref)], sems)
    for side, x in enumerate((0, size_x - 1)):
        copies += fetch(
            [(first_hbm.at[pl.ds(x * size_y, size_y)], send_ref.at[side, pl.ds(0, size_y)])], sems, 2 + side
        )
    wait(copies)
    for side, x in enumerate((0, size_x - 1)):
        send_ref[side, size_y : size_y + 1] = yhi_ref[x : x + 1, :]
        send_ref[side, size_y + 7 : size_y + 8] = ylo_ref[x : x + 1, :]
    wait(fetch([(send_ref.at[0], below_hbm), (send_ref.at[1], above_hbm)], sems))


def field_kernel(
    owner_ref, first_hbm, cond_hbm, rate_hbm, total_hbm, reft_hbm, expand_hbm,
    xlo_hbm, xhi_hbm, krim_hbm, ylo_hbm, yhi_hbm, fxlo_hbm, fxhi_hbm,
    field_hbm, late_hbm,
    first_ref, cond_ref, rate_ref, total_ref, reft_ref, expand_ref, field_ref, stage_ref,
    outer_ref, rim_ref, ylo_ref, yhi_ref, planes_ref,
    ex_ref, ey_ref, ez_ref, sv_ref, pv_ref, sems, late_sem,
    *, size_x, size_y, tile_rows, early_rows, groups,
):
    copies = fetch(
        [(ylo_hbm, ylo_ref), (yhi_hbm, yhi_ref), (krim_hbm, rim_ref),
         (xlo_hbm, outer_ref.at[0]), (xhi_hbm, outer_ref.at[1]),
         (fxlo_hbm, planes_ref.at[0]), (fxhi_hbm, planes_ref.at[1])], sems,
    )
    rows = first_ref.shape[0] // groups
    part = lambda g: pl.ds(g * rows, rows)
    loads = [
        fetch([(first_hbm.at[part(g)], first_ref.at[part(g)]), (cond_hbm.at[:, part(g)], cond_ref.at[:, part(g)])],
              sems, 7 + 2 * g)
        for g in range(groups)
    ]
    later = fetch(
        [(rate_hbm, rate_ref), (total_hbm, total_ref), (reft_hbm, reft_ref), (expand_hbm, expand_ref)],
        sems, 7 + 2 * groups,
    )
    wait(copies)
    set_rim(rim_ref, 0, ylo_ref, yhi_ref, size_x)
    refs = (ex_ref, ey_ref, ez_ref, sv_ref)
    for side, x in enumerate((0, size_x + 1)):
        tiles = [split(planes_ref[side])]
        tiles += [with_rim(rim_ref, f, outer_ref[side, f], x) for f in range(1, 4)]
        plane_terms(tiles, x, refs, True)

    def first_pass(x, carry):
        at = pl.ds(pl.multiple_of(x * size_y, size_y), size_y)
        values = [first_ref[at, :]] + [cond_ref[f, at, :] for f in range(3)]
        tiles = [with_rim(rim_ref, f, values[f], x + 1) for f in range(4)]
        put(pv_ref, x, plane_terms(tiles, x + 1, refs))
        return carry

    each_group = size_x // groups
    for g in range(groups):
        wait(loads[g])
        lax.fori_loop(g * each_group, (g + 1) * each_group, first_pass, 0)
    wait(later)
    per_plane = size_y // tile_rows
    kept = tile_rows - early_rows

    def second_pass(x, carry):
        at = pl.ds(pl.multiple_of(x * size_y, size_y), size_y)
        k = [cond_ref[f, at, :] for f in range(3)]
        h = coupled(k, pv_ref[x], [r.at[x] for r in refs], [r.at[x + 2] for r in refs])
        field = (1.0 - OMEGA) * first_ref[at, :] + total_ref[at, :] + (0.5 * rate_ref[at, :]) * h
        field_ref[at, :] = field
        strain = field - reft_ref[at, :]
        for p in range(per_plane):
            tile = x * per_plane + p
            start = p * tile_rows
            early, end = start + early_rows, start + tile_rows
            if early_rows:
                stage_ref[tile, :early_rows] = strain[start:early]
            for c in range(3 if kept else 0):
                low = early_rows + c * kept
                stage_ref[tile, low : low + kept] = (expand_ref[c, at, :] * strain)[early:end]
            pltpu.make_async_copy(stage_ref.at[tile], late_hbm.at[owner_ref[0, tile]], late_sem).start()
        return carry

    sent = []
    for g in range(groups):
        lax.fori_loop(g * each_group, (g + 1) * each_group, second_pass, 0)
        sent += fetch([(field_ref.at[part(g)], field_hbm.at[part(g)])], sems, g)
    wait(sent)
    pltpu.make_async_copy(stage_ref, late_hbm, late_sem).wait()


def early_kernel(owner_ref, expand_hbm, out_hbm, stage_ref, in_sems, sem, *, tile_rows, early_rows, groups):
    tiles = stage_ref.shape[0] // groups
    loads = []
    for g in range(groups):
        for j in range(g * tiles, (g + 1) * tiles):
            loads.append(
                pltpu.make_async_copy(
                    expand_hbm.at[:, pl.ds(j * tile_rows, early_rows)], stage_ref.at[j], in_sems.at[g]
                )
            )
            loads[-1].start()
    for g in range(groups):
        wait(loads[g * tiles : (g + 1) * tiles])
        for j in range(g * tiles, (g + 1) * tiles):
            pltpu.make_async_copy(stage_ref.at[j], out_hbm.at[owner_ref[0, j]], sem).start()
    pltpu.make_async_copy(stage_ref, out_hbm, sem).wait()


def settle_kernel(*refs, tile_rows, early_rows, pieces):
    late, early, out_ref = refs[:pieces], refs[pieces:-1], refs[-1]
    kept = tile_rows - early_rows
    pitch = early_rows + 3 * kept
    lane = lambda y, p: slice((y * pieces + p) * LANES, (y * pieces + p + 1) * LANES)
    for p in range(pieces):
        for y in range(early_rows):
            strain = late[p][pl.ds(y, 8, stride=pitch), :]
            for c in range(3):
                factor = early[p][pl.ds(c * early_rows + y, 8, stride=3 * early_rows), :]
                out_ref[0, c, :, lane(y, p)] = factor * strain
        for c in range(3):
            for y in range(kept):
                at = early_rows + c * kept + y
                out_ref[0, c, :, lane(early_rows + y, p)] = late[p][pl.ds(at, 8, stride=pitch), :]


def neighbours(axis):
    count = lax.axis_size(axis)
    up = [(i, i + 1) for i in range(count - 1)]
    return up, [(b, a) for a, b in up]


def body(
    adjoint_temp, adjoint_load, conductivity, expansion, ref_temp,
    wall_rows, wall_dest, wall_line, wall_count, tile_owner,
):
    devices = lax.axis_size("gx") * lax.axis_size("gy")
    size_x, size_y, size_z = adjoint_temp.shape
    rows_dev, width = wall_rows.shape
    cells = size_x * size_y
    pieces = size_z // LANES
    capacity = (rows_dev + devices - 1) // devices + 1
    pitch = (capacity + 1 + CORNER_ROWS * pieces + 7) // 8 * 8
    tile_rows = cells // devices
    early_rows = tile_rows // 8 * EARLY_EIGHTHS // 8 * 8
    kept = tile_rows - early_rows
    up_x, down_x = neighbours("gx")
    up_y, down_y = neighbours("gy")
    exchange = lambda array: lax.all_to_all(array, AXES, split_axis=0, concat_axis=0, tiled=True)
    flat = lambda array: array.reshape(array.shape[:-3] + (cells, size_z))
    temp, cond, load, expand = map(flat, (adjoint_temp, conductivity, adjoint_load, expansion))

    buffer = lambda *dims: pltpu.VMEM(dims, F32)
    sems = lambda count: pltpu.SemaphoreType.DMA((count,))
    grid, lines = shape(cells, size_z), shape(size_x, size_z)

    packed, below, above, low, high = call(
        lambda *refs: prepare_kernel(
            *refs, devices=devices, capacity=capacity, pitch=pitch, size_x=size_x, size_y=size_y
        ),
        (shape(devices * pitch, width),) + (shape(4, size_y, size_z),) * 2 + (shape(4, size_x, size_z),) * 2,
        scratch=[
            buffer(rows_dev, width), pltpu.VMEM((1, rows_dev), jnp.int32),
            pltpu.VMEM((1, rows_dev), jnp.int32), buffer(2, 4, size_y, size_z),
            buffer(2, 4, size_x, 8, size_z), buffer(devices * pitch, width),
            buffer(4, size_x, size_z), buffer(4, size_x, size_z), sems(19),
        ],
        specs=whole(1, SMEM) + whole(5, HBM),
        limit=60,
    )(wall_count, wall_rows, wall_dest.reshape(1, rows_dev), wall_line.reshape(1, rows_dev),
      adjoint_temp, conductivity)
    got = exchange(packed.reshape(devices, pitch, width)).reshape(devices * pitch, width)
    ylo = lax.ppermute(high, "gy", up_y)
    yhi = lax.ppermute(low, "gy", down_y)
    xlo = lax.ppermute(above, "gx", up_x)
    xhi = lax.ppermute(below, "gx", down_x)

    early = None
    if early_rows:
        early = call(
            lambda *refs: early_kernel(*refs, tile_rows=tile_rows, early_rows=early_rows, groups=1),
            shape(devices, 3, early_rows, size_z),
            scratch=[buffer(devices, 3, early_rows, size_z), sems(1), pltpu.SemaphoreType.DMA(())],
            specs=whole(1, SMEM) + whole(1, HBM),
        )(tile_owner, expand)
        early = exchange(early)

    rim_rows = (size_x + 2) * 8
    wide = buffer(size_x + 2, size_y, size_z)
    plane, flat_plane = buffer(size_x, size_y, size_z), buffer(cells, size_z)
    stack, rims = buffer(3, cells, size_z), (4, pieces, rim_rows, LANES)
    first_call = call(
        lambda *refs: first_kernel(
            *refs, devices=devices, size_x=size_x, size_y=size_y, capacity=capacity, pitch=pitch,
            step=cells // 8, groups=GROUPS,
        ),
        (grid, grid, grid, shape(*rims), lines, lines),
        scratch=[flat_plane, stack] + [flat_plane] * 4 + [buffer(*rims)] + [buffer(size_x, size_z)] * 2
        + [wide] * 5 + [plane] * 2 + [
            buffer(2, 4, size_y, size_z), buffer(4, size_x, size_z), buffer(4, size_x, size_z),
            buffer(devices * pitch, width), pltpu.VMEM((devices * pitch, 2 * width), BF16),
            buffer(pieces, cells, LANES), sems(6 + 4 * GROUPS),
        ],
        specs=whole(8, HBM),
        limit=60,
    )
    first, total, rate, krim, low, high = first_call(temp, cond, load, xlo, xhi, ylo, yhi, got)
    fylo = lax.ppermute(high, "gy", up_y)
    fyhi = lax.ppermute(low, "gy", down_y)
    sides = [buffer(size_x, size_z)] * 2
    edge = shape(size_y + 8, size_z)
    below, above = call(
        lambda *refs: planes_kernel(*refs, size_x=size_x, size_y=size_y),
        (edge, edge),
        scratch=sides + [buffer(2, size_y + 8, size_z), sems(4)],
        specs=whole(3, HBM),
    )(first, fylo, fyhi)
    fxlo = lax.ppermute(above, "gx", up_x)
    fxhi = lax.ppermute(below, "gx", down_x)

    late_rows = early_rows + 3 * kept
    field, late = call(
        lambda *refs: field_kernel(
            *refs, size_x=size_x, size_y=size_y, tile_rows=tile_rows, early_rows=early_rows,
            groups=GROUPS,
        ),
        (grid, shape(devices, late_rows, size_z)),
        scratch=[flat_plane, stack] + [flat_plane] * 3 + [stack, flat_plane]
        + [buffer(devices, late_rows, size_z), buffer(2, 4, size_y, size_z), buffer(*rims)] + sides
        + [buffer(2, size_y + 8, size_z)] + [wide] * 4 + [plane]
        + [sems(11 + 2 * GROUPS), pltpu.SemaphoreType.DMA(())],
        specs=whole(1, SMEM) + whole(13, HBM),
        limit=60,
    )(tile_owner, first, cond, rate, total, flat(ref_temp), expand, xlo, xhi, krim, fylo, fyhi, fxlo, fxhi)

    moved = exchange(late)
    tile_cells = tile_rows * size_z
    received = [(moved.reshape(devices * late_rows, size_z), late_rows)]
    if early_rows:
        received.append((early.reshape(devices * 3 * early_rows, size_z), 3 * early_rows))
    block_load = pl.pallas_call(
        lambda *refs: settle_kernel(*refs, tile_rows=tile_rows, early_rows=early_rows, pieces=pieces),
        out_shape=shape(1, 3, devices, tile_cells),
        grid=(devices // 8,),
        in_specs=[
            pl.BlockSpec((8 * rows, LANES), lambda b, p=p: (b, p)) for _, rows in received for p in range(pieces)
        ],
        out_specs=pl.BlockSpec((1, 3, 8, tile_cells), lambda b: (0, 0, b, 0)),
        compiler_params=pltpu.CompilerParams(vmem_limit_bytes=12 * MIB),
        name="settle",
    )(*[array for array, _ in received for _ in range(pieces)])
    return field.reshape(size_x, size_y, size_z), block_load


def solution(mesh):
    placed = (
        P("gx", "gy", None),
        P("gx", "gy", None),
        P(None, "gx", "gy", None),
        P(None, "gx", "gy", None),
        P("gx", "gy", None),
        P(("gx", "gy"), None),
        P(("gx", "gy"), None),
        P(("gx", "gy")),
        P(("gx", "gy")),
        P(("gx", "gy"), None),
    )

    return jax.shard_map(
        body,
        mesh=mesh,
        in_specs=placed,
        out_specs=(P("gx", "gy", None), P(("gx", "gy"), None, None, None)),
        check_vma=False,
    )
```

time: 165 us -> 154 us (0.933)
  local copies, waits for them, and re-layouts: 20 us -> 1.96 us
  waiting for transfers between devices: 3.39 us -> 20.9 us
  blocking collectives: 84.2 us -> 69.9 us
  Pallas kernels: 24.6 us -> 29.4 us
    all_to_all x1, blocking collectives: 84.2 us -> 69.9 us  [body(): lax.all_to_all(array, AXES, split_axis=0, concat_axis=0, tiled=True)]
    unnamed x40 -> x26, local copies, waits for them, and re-layouts: 14.6 us -> 1.96 us
    ppermute x8, waiting for transfers between devices: 3.38 us -> 13.6 us  [the longest x1 5.55 us: body(): xhi = lax.ppermute(below, 'gx', down_x)]
    all_to_all x1 -> x2, waiting for transfers between devices: 0.01 us -> 7.31 us  [body(): lax.all_to_all(array, AXES, split_axis=0, concat_axis=0, tiled=True)]
    pallas_call x5 -> x6, Pallas kernels: 24.6 us -> 29.4 us  [the longest x1 11.3 us: body(): first_call(temp, cond, load, xlo, xhi, ylo, yhi, got)]
    slice x9 -> x0, local copies, waits for them, and re-layouts: 4.35 us -> none  [the longest x1 1.52 us: edge(): conductivity[:, :, at]]
    all_to_all x1 -> x2, starting transfers between devices: 7.65 us -> 10.2 us  [body(): lax.all_to_all(array, AXES, split_axis=0, concat_axis=0, tiled=True)]
    ppermute x8, starting transfers between devices: 21.7 us -> 19.2 us  [the longest x1 4.61 us: body(): fxlo = lax.ppermute(above, 'gx', up_x)]
  transfers between devices with their start and end apart: 9 -> 10, of which waited for: 3 -> 6; matrix products, arithmetic and copies ran while one was open for 3% -> 0% of each run, Pallas kernels for 5% -> 16%
where the time goes in v2:
time: 154 us; the launch traced here: 153 us
  blocking collectives  69.9 us (45%)
  starting transfers between devices  29.5 us (19%)
  Pallas kernels  29.4 us (19%)
  waiting for transfers between devices  20.9 us (14%)
  local copies, waits for them, and re-layouts  1.96 us (1%)
    all_to_all x1, blocking collectives, body(): lax.all_to_all(array, AXES, split_axis=0, concat_axis=0, tiled=True)  69.9 us
    pallas_call x1, Pallas kernels, body(): first_call(temp, cond, load, xlo, xhi, ylo, yhi, got)  11.3 us
    all_to_all x2, starting transfers between devices, body(): lax.all_to_all(array, AXES, split_axis=0, concat_axis=0, tiled=True)  10.2 us
    pallas_call x1, Pallas kernels, body(): call(lambda *refs: field_kernel(*refs, size_x=size_x, size_y=size_y, tile...  8.52 us
    all_to_all x2, waiting for transfers between devices, body(): lax.all_to_all(array, AXES, split_axis=0, concat_axis=0, tiled=True)  7.31 us
    ppermute x1, waiting for transfers between devices, body(): xhi = lax.ppermute(below, 'gx', down_x)  5.55 us
    ppermute x1, starting transfers between devices, body(): fxlo = lax.ppermute(above, 'gx', up_x)  4.61 us
    ppermute x1, waiting for transfers between devices, body(): fxhi = lax.ppermute(below, 'gx', down_x)  4.13 us
  transfers between devices with their start and end apart: 10, of which 6 were waited for; matrix products, arithmetic and copies ran while one was open for 0% of the time, Pallas kernels for 16%

profile of v2, /device:TPU:0, one launch (start us, length us, event | category | flops | bytes accessed | tf_op | source)
XLA Modules:
  0.0 153.1 jit_solution(14044053121536649166)
XLA Ops:
  1.3 2.8 %shard_map.113 = (f32[512,128]{1,0:T(8,128)}, f32[4,32,256]{2,1,0:T(8,128)}, f32[4,32,256]{2,1,0:T(8,128)}, f32[4,32,256]{2,1,0:T(8,128)}, f32[4,32,256]{2,1,0:T(8,128)}) custom-call(s32[1]{0:T(128)S(6)} %copy.12.refs_0_, f32[256,128]{1,0:T(8,128)} %refs_1_.1, s32[1,256]{1,0:T(1,128)} %bitcast.25, s32[1,256]{1,0:T(1,128)} %bitcast.26, ...), custom_call_target="tpu_custom_call" | custom-call | tf_op jit(solution)/shard_map/pallas_call | solution.py:511
  4.1 0.0 copy-start.11
  4.1 7.3 %all-to-all-start = ((f32[32,16,128]{2,1,0:T(8,128)}), f32[32,16,128]{2,1,0:T(8,128)S(1)}, u32[]{:S(2)}, u32[]{:S(2)}) async-start(f32[32,16,128]{2,1,0:T(8,128)} %bitcast.24), calls=%async_computation | async-start | bytes 524288 | tf_op jit(solution)/shard_map/all_to_all | solution.py:503
  11.4 2.7 %shard_map.117 = f32[32,3,8,256]{3,2,1,0:T(8,128)} custom-call(s32[1,32]{1,0:T(1,128)} %refs_0_.4, f32[3,1024,256]{2,1,0:T(8,128)} %bitcast.18), custom_call_target="tpu_custom_call" | custom-call | tf_op jit(solution)/shard_map/pallas_call | solution.py:534
  14.1 7.3 %all-to-all-done = f32[32,16,128]{2,1,0:T(8,128)S(1)} async-done(((f32[32,16,128]{2,1,0:T(8,128)}), f32[32,16,128]{2,1,0:T(8,128)S(1)}, u32[]{:S(2)}, u32[]{:S(2)}) %all-to-all-start) | async-done | bytes 262176 | tf_op jit(solution)/shard_map/all_to_all | solution.py:503
  21.4 2.9 %all-to-all-start.2 = ((f32[32,3,8,256]{3,2,1,0:T(8,128)}), f32[32,3,8,256]{3,2,1,0:T(8,128)S(1)}, u32[]{:S(2)}, u32[]{:S(2)}) async-start(f32[32,3,8,256]{3,2,1,0:T(8,128)} %shard_map.117), calls=%async_computation.2 | async-start | bytes 1572864 | tf_op jit(solution)/shard_map/all_to_all | solution.py:503
  24.3 3.7 %collective-permute-start = (f32[4,32,256]{2,1,0:T(8,128)S(1)}, f32[4,32,256]{2,1,0:T(8,128)S(1)}, u32[]{:S(2)}, u32[]{:S(2)}) collective-permute-start(f32[4,32,256]{2,1,0:T(8,128)S(1)} %copy-done.12), channel_id=1, source_target_pairs={{0,8},{8,16},{16,24},{1,9},{9,17},{17,25},{2,10},{10,18},{18,26},{... | collective-permute-start | bytes 393224 | tf_op jit(solution)/shard_map/ppermute | solution.py:529
  28.0 1.3 collective-permute-start.1
  29.3 1.7 %collective-permute-start.2 = (f32[4,32,256]{2,1,0:T(8,128)S(1)}, f32[4,32,256]{2,1,0:T(8,128)S(1)}, u32[]{:S(2)}, u32[]{:S(2)}) collective-permute-start(f32[4,32,256]{2,1,0:T(8,128)S(1)} %copy-done.10), channel_id=1, source_target_pairs={{0,1},{1,2},{2,3},{3,4},{4,5},{5,6},{6,7},{8,9},{9,10},{10,11},{11... | collective-permute-start | bytes 393224 | tf_op jit(solution)/shard_map/ppermute | solution.py:527
  31.1 1.3 collective-permute-start.3
  32.4 1.2 collective-permute-done.refs_3_.refs_7_
  33.7 5.6 %collective-permute-done.1.refs_4_.refs_8_ = f32[4,32,256]{2,1,0:T(8,128)S(1)} collective-permute-done((f32[4,32,256]{2,1,0:T(8,128)S(1)}, f32[4,32,256]{2,1,0:T(8,128)S(1)}, u32[]{:S(2)}, u32[]{:S(2)}) %collective-permute-start.1) | collective-permute-done | bytes 131104 | tf_op jit(solution)/shard_map/ppermute | solution.py:530
  39.2 0.0 collective-permute-done.2.refs_5_
  39.2 0.0 collective-permute-done.3.refs_6_
  39.3 0.6 copy-done.2
  39.9 0.0 copy-done.5
  39.9 0.0 copy-done.6
  40.0 11.3 %shard_map.114 = (f32[1024,256]{1,0:T(8,128)}, f32[1024,256]{1,0:T(8,128)}, f32[1024,256]{1,0:T(8,128)}, f32[4,2,272,128]{3,2,1,0:T(8,128)}, f32[32,256]{1,0:T(8,128)}, /*index=5*/f32[32,256]{1,0:T(8,128)}) custom-call(f32[1024,256]{1,0:T(8,128)} %bitcast.20, f32[3,1024,256]{2,1,0:T(8,128)} %bitcast.16, f32[1024,256]{1,0:T(8,128)} %bitcast.23, ...), custom_call_target="tpu_custom_call" | custom-call | tf_op jit(solution)/shard_map/pallas_call | solution.py:561
  51.2 4.0 %collective-permute-start.4 = (f32[32,256]{1,0:T(8,128)}, f32[32,256]{1,0:T(8,128)S(1)}, u32[]{:S(2)}, u32[]{:S(2)}) collective-permute-start(f32[32,256]{1,0:T(8,128)} %get-tuple-element.26), channel_id=1, source_target_pairs={{0,1},{1,2},{2,3},{3,4},{4,5},{5,6},{6,7},{8,9},{9,10},{10,11},{11... | collective-permute-start | bytes 98312 | tf_op jit(solution)/shard_map/ppermute | solution.py:562
  55.3 1.3 collective-permute-start.5
  56.6 0.0 collective-permute-done.4.refs_1_.refs_10_
  56.6 2.0 %collective-permute-done.5.refs_2_.refs_11_ = f32[32,256]{1,0:T(8,128)S(1)} collective-permute-done((f32[32,256]{1,0:T(8,128)}, f32[32,256]{1,0:T(8,128)S(1)}, u32[]{:S(2)}, u32[]{:S(2)}) %collective-permute-start.5) | collective-permute-done | bytes 32800 | tf_op jit(solution)/shard_map/ppermute | solution.py:563
  58.6 0.6 copy-done.4
  59.2 1.5 shard_map.115
  60.7 4.6 %collective-permute-start.6 = (f32[40,256]{1,0:T(8,128)}, f32[40,256]{1,0:T(8,128)S(1)}, u32[]{:S(2)}, u32[]{:S(2)}) collective-permute-start(f32[40,256]{1,0:T(8,128)} %get-tuple-element.28), channel_id=1, source_target_pairs={{0,8},{8,16},{16,24},{1,9},{9,17},{17,25},{2,10},{10,18},{18,26},{... | collective-permute-start | bytes 122888 | tf_op jit(solution)/shard_map/ppermute | solution.py:572
  65.3 1.3 collective-permute-start.7
  66.6 0.7 collective-permute-done.6.refs_12_
  67.3 4.1 %collective-permute-done.7.refs_13_ = f32[40,256]{1,0:T(8,128)S(1)} collective-permute-done((f32[40,256]{1,0:T(8,128)}, f32[40,256]{1,0:T(8,128)S(1)}, u32[]{:S(2)}, u32[]{:S(2)}) %collective-permute-start.7) | collective-permute-done | bytes 40992 | tf_op jit(solution)/shard_map/ppermute | solution.py:573
  71.4 0.6 copy-done.8
  72.0 8.5 %shard_map.116 = (f32[1024,256]{1,0:T(8,128)}, f32[32,80,256]{2,1,0:T(8,128)}) custom-call(s32[1,32]{1,0:T(1,128)} %refs_0_.4, f32[1024,256]{1,0:T(8,128)} %get-tuple-element.22.refs_0_.refs_1_, f32[3,1024,256]{2,1,0:T(8,128)} %bitcast.17, f32[1024,256]{1,0:T(8,128)} %get-tuple-element.23.refs_3_, f32[1024,256]{1,0:T(8,128)} %get-tuple-element.24.refs_4_, ...), custom_call_target="tpu_custom_call" | custom-call | tf_op jit(solution)/shard_map/pallas_call | solution.py:576
  80.6 69.9 %all_to_all.15 = f32[32,80,256]{2,1,0:T(8,128)S(1)} all-to-all(f32[32,80,256]{2,1,0:T(8,128)} %get-tuple-element.31), channel_id=1, replica_groups=mesh['gx'=4,'gy'=8] {'gx','gy'}, dimensions={0} | all-to-all | bytes 5242880 | tf_op jit(solution)/shard_map/all_to_all | solution.py:503
  150.4 2.7 %settle.1 = f32[1,3,32,8192]{3,2,1,0:T(8,128)} custom-call(f32[2560,256]{1,0:T(8,128)S(1)} %bitcast.12, f32[2560,256]{1,0:T(8,128)S(1)} %bitcast.13, f32[768,256]{1,0:T(8,128)S(1)} %bitcast.14, f32[768,256]{1,0:T(8,128)S(1)} %bitcast.15), custom_call_target="tpu_custom_call" | custom-call | tf_op jit(solution)/shard_map/settle/pallas_call | solution.py:595
  (21 shorter events, 0.0 us)
Async XLA Ops:
  4.1 20.3 %copy-start.12 = (f32[4,32,256]{2,1,0:T(8,128)S(1)}, f32[4,32,256]{2,1,0:T(8,128)}, u32[]{:S(2)}) copy-start(f32[4,32,256]{2,1,0:T(8,128)} %get-tuple-element.17) | copy-start | bytes 393220
  4.1 24.0 %copy-start.11 = (f32[4,32,256]{2,1,0:T(8,128)S(1)}, f32[4,32,256]{2,1,0:T(8,128)}, u32[]{:S(2)}) copy-start(f32[4,32,256]{2,1,0:T(8,128)} %get-tuple-element.18) | copy-start | bytes 393220
  4.1 25.3 %copy-start.10 = (f32[4,32,256]{2,1,0:T(8,128)S(1)}, f32[4,32,256]{2,1,0:T(8,128)}, u32[]{:S(2)}) copy-start(f32[4,32,256]{2,1,0:T(8,128)} %get-tuple-element.19) | copy-start | bytes 393220
  4.1 27.0 %copy-start.9 = (f32[4,32,256]{2,1,0:T(8,128)S(1)}, f32[4,32,256]{2,1,0:T(8,128)}, u32[]{:S(2)}) copy-start(f32[4,32,256]{2,1,0:T(8,128)} %get-tuple-element.20) | copy-start | bytes 393220
  4.1 17.3 %all-to-all-start = ((f32[32,16,128]{2,1,0:T(8,128)}), f32[32,16,128]{2,1,0:T(8,128)S(1)}, u32[]{:S(2)}, u32[]{:S(2)}) async-start(f32[32,16,128]{2,1,0:T(8,128)} %bitcast.24), calls=%async_computation | async-start | bytes 524288 | tf_op jit(solution)/shard_map/all_to_all | solution.py:503
  21.4 17.8 %copy-start = (f32[32,16,128]{2,1,0:T(8,128)}, f32[32,16,128]{2,1,0:T(8,128)S(1)}, u32[]{:S(2)}) copy-start(f32[32,16,128]{2,1,0:T(8,128)S(1)} %all-to-all-done) | copy-start | bytes 786436
  21.4 59.1 %all-to-all-start.2 = ((f32[32,3,8,256]{3,2,1,0:T(8,128)}), f32[32,3,8,256]{3,2,1,0:T(8,128)S(1)}, u32[]{:S(2)}, u32[]{:S(2)}) async-start(f32[32,3,8,256]{3,2,1,0:T(8,128)} %shard_map.117), calls=%async_computation.2 | async-start | bytes 1572864 | tf_op jit(solution)/shard_map/all_to_all | solution.py:503
  24.3 9.3 %collective-permute-start = (f32[4,32,256]{2,1,0:T(8,128)S(1)}, f32[4,32,256]{2,1,0:T(8,128)S(1)}, u32[]{:S(2)}, u32[]{:S(2)}) collective-permute-start(f32[4,32,256]{2,1,0:T(8,128)S(1)} %copy-done.12), channel_id=1, source_target_pairs={{0,8},{8,16},{16,24},{1,9},{9,17},{17,25},{2,10},{10,18},{18,26},{... | collective-permute-start | bytes 393224 | tf_op jit(solution)/shard_map/ppermute | solution.py:529
  28.0 11.2 %collective-permute-start.1 = (f32[4,32,256]{2,1,0:T(8,128)S(1)}, f32[4,32,256]{2,1,0:T(8,128)S(1)}, u32[]{:S(2)}, u32[]{:S(2)}) collective-permute-start(f32[4,32,256]{2,1,0:T(8,128)S(1)} %copy-done.11), channel_id=1, source_target_pairs={{8,0},{16,8},{24,16},{9,1},{17,9},{25,17},{10,2},{18,10},{26,18},{... | collective-permute-start | bytes 393224 | tf_op jit(solution)/shard_map/ppermute | solution.py:530
  29.3 9.9 %collective-permute-start.2 = (f32[4,32,256]{2,1,0:T(8,128)S(1)}, f32[4,32,256]{2,1,0:T(8,128)S(1)}, u32[]{:S(2)}, u32[]{:S(2)}) collective-permute-start(f32[4,32,256]{2,1,0:T(8,128)S(1)} %copy-done.10), channel_id=1, source_target_pairs={{0,1},{1,2},{2,3},{3,4},{4,5},{5,6},{6,7},{8,9},{9,10},{10,11},{11... | collective-permute-start | bytes 393224 | tf_op jit(solution)/shard_map/ppermute | solution.py:527
  31.1 8.1 %collective-permute-start.3 = (f32[4,32,256]{2,1,0:T(8,128)S(1)}, f32[4,32,256]{2,1,0:T(8,128)S(1)}, u32[]{:S(2)}, u32[]{:S(2)}) collective-permute-start(f32[4,32,256]{2,1,0:T(8,128)S(1)} %copy-done.9), channel_id=1, source_target_pairs={{1,0},{2,1},{3,2},{4,3},{5,4},{6,5},{7,6},{9,8},{10,9},{11,10},{12... | collective-permute-start | bytes 393224 | tf_op jit(solution)/shard_map/ppermute | solution.py:528
  33.7 5.6 %copy-start.1 = (f32[4,32,256]{2,1,0:T(8,128)}, f32[4,32,256]{2,1,0:T(8,128)S(1)}, u32[]{:S(2)}) copy-start(f32[4,32,256]{2,1,0:T(8,128)S(1)} %collective-permute-done.refs_3_.refs_7_) | copy-start | bytes 393220
  39.2 0.7 copy-start.2
  39.2 0.7 copy-start.5
  39.2 0.7 copy-start.6
  51.2 5.4 %collective-permute-start.4 = (f32[32,256]{1,0:T(8,128)}, f32[32,256]{1,0:T(8,128)S(1)}, u32[]{:S(2)}, u32[]{:S(2)}) collective-permute-start(f32[32,256]{1,0:T(8,128)} %get-tuple-element.26), channel_id=1, source_target_pairs={{0,1},{1,2},{2,3},{3,4},{4,5},{5,6},{6,7},{8,9},{9,10},{10,11},{11... | collective-permute-start | bytes 98312 | tf_op jit(solution)/shard_map/ppermute | solution.py:562
  55.3 3.3 %collective-permute-start.5 = (f32[32,256]{1,0:T(8,128)}, f32[32,256]{1,0:T(8,128)S(1)}, u32[]{:S(2)}, u32[]{:S(2)}) collective-permute-start(f32[32,256]{1,0:T(8,128)} %get-tuple-element.27), channel_id=1, source_target_pairs={{1,0},{2,1},{3,2},{4,3},{5,4},{6,5},{7,6},{9,8},{10,9},{11,10},{12... | collective-permute-start | bytes 98312 | tf_op jit(solution)/shard_map/ppermute | solution.py:563
  56.6 2.0 %copy-start.3 = (f32[32,256]{1,0:T(8,128)}, f32[32,256]{1,0:T(8,128)S(1)}, u32[]{:S(2)}) copy-start(f32[32,256]{1,0:T(8,128)S(1)} %collective-permute-done.4.refs_1_.refs_10_) | copy-start | bytes 98308
  58.6 0.6 copy-start.4
  60.7 6.6 %collective-permute-start.6 = (f32[40,256]{1,0:T(8,128)}, f32[40,256]{1,0:T(8,128)S(1)}, u32[]{:S(2)}, u32[]{:S(2)}) collective-permute-start(f32[40,256]{1,0:T(8,128)} %get-tuple-element.28), channel_id=1, source_target_pairs={{0,8},{8,16},{16,24},{1,9},{9,17},{17,25},{2,10},{10,18},{18,26},{... | collective-permute-start | bytes 122888 | tf_op jit(solution)/shard_map/ppermute | solution.py:572
  65.3 6.1 %collective-permute-start.7 = (f32[40,256]{1,0:T(8,128)}, f32[40,256]{1,0:T(8,128)S(1)}, u32[]{:S(2)}, u32[]{:S(2)}) collective-permute-start(f32[40,256]{1,0:T(8,128)} %get-tuple-element.29), channel_id=1, source_target_pairs={{8,0},{16,8},{24,16},{9,1},{17,9},{25,17},{10,2},{18,10},{26,18},{... | collective-permute-start | bytes 122888 | tf_op jit(solution)/shard_map/ppermute | solution.py:573
  67.3 4.1 %copy-start.7 = (f32[40,256]{1,0:T(8,128)}, f32[40,256]{1,0:T(8,128)S(1)}, u32[]{:S(2)}) copy-start(f32[40,256]{1,0:T(8,128)S(1)} %collective-permute-done.6.refs_12_) | copy-start | bytes 122884
  71.4 0.6 copy-start.8
